TPU v7x, 128 devices: a whole 4x4x4 slice. The times are simulated.
128 devices in a mesh: rows: 16 (over x, z_hi, core), cols: 8 (over y, z_lo).
Axes of the slice: x: 4, y: 4, z: 4 (z_hi: 2, z_lo: 2; z = z_hi * 2 + z_lo), core: 2. Of those that a mesh axis runs over, the one named last changes fastest.
Arguments:
- bottleneck: bfloat16 [8, 256, 16, 256], P(None, None, 'rows', 'cols'), may hold values from -8 to 8
- skip_field: bfloat16 [8, 128, 32, 512], P(None, None, 'rows', 'cols'), may hold values from -6 to 6
- cotangent: bfloat16 [8, 128, 32, 512], P(None, None, 'rows', 'cols'), may hold values from -6 to 6
- noise_level: int32 [8], replicated, may hold values from 0 to 17
- qkv_weight: bfloat16 [768, 256], replicated, may hold values from -0.5 to 0.5
- out_weight: bfloat16 [256, 256], replicated, may hold values from -3 to 3
- up_weight: bfloat16 [128, 256], replicated, may hold values from -0.375 to 0.375
- conv_weight: bfloat16 [9, 128, 128], replicated, may hold values from -0.1875 to 0.1875
- film_scale: float32 [18, 128], replicated, may hold values from -2 to 2
- film_shift: float32 [18, 128], replicated, may hold values from -2 to 2
Outputs:
- decoded: bfloat16 [8, 128, 32, 512], P(None, None, 'rows', 'cols')
- grad_bottleneck: float32 [8, 256, 16, 256], P(None, None, 'rows', 'cols')
- grad_skip: bfloat16 [8, 128, 32, 512], P(None, None, 'rows', 'cols')
- grad_qkv: float32 [768, 256], replicated
- grad_out: float32 [256, 256], replicated
- grad_up: float32 [128, 256], replicated
- grad_conv: float32 [9, 128, 128], replicated
- grad_scale: float32 [18, 128], replicated
- grad_shift: float32 [18, 128], replicated
All inputs are finite; a program needn't handle non-finite values.
Results may differ from a plain program's by a relative error of at most 0.023.
The roundings to bfloat16 on the way count: a program that leaves them out, or rounds other values in their place, can miss the bound.
Values may be sent and summed in bfloat16 or wider, within the bound.
A program may use at most 64 MiB of HBM per device.

v0:
```python
import math

import jax
import jax.numpy as jnp
from jax import lax
from jax.sharding import PartitionSpec as P

HEAD_DIM = 64


OFFSETS = [(-1, -1), (-1, 0), (-1, 1), (0, -1), (0, 0), (0, 1), (1, -1), (1, 0), (1, 1)]


def with_halo(cells, sides, width):
    for axis, dim in sides:
        count = lax.axis_size(axis)
        ends = count - 1
        head = lax.slice_in_dim(cells, 0, width, axis=dim)
        tail = lax.slice_in_dim(cells, cells.shape[dim] - width, cells.shape[dim], axis=dim)
        cells = jnp.concatenate(
            [
                lax.ppermute(tail, axis, [(i, (i + 1) % count) for i in range(ends)]),
                cells,
                lax.ppermute(head, axis, [((i + 1) % count, i) for i in range(ends)]),
            ],
            axis=dim,
        )
    return cells


def packed_total(arrays, axis):
    flat, at, gathered = (jnp.concatenate([a.reshape(-1) for a in arrays]), 0, [])
    so_far = lax.psum(flat, axis)
    for a in arrays:
        gathered.append(so_far[at : at + a.size].reshape(a.shape))
        at += a.size
    return tuple(gathered)


def on_device(
    bottleneck,
    skip_field,
    cotangent,
    noise_level,
    qkv_weight,
    out_weight,
    up_weight,
    conv_weight,
    film_scale,
    film_shift,
):
    batch, channels, tile_rows, tile_cols = bottleneck.shape
    narrow = up_weight.shape[0]
    heads = channels // HEAD_DIM
    factor = 1.0 / math.sqrt(HEAD_DIM)
    levels = film_scale.shape[0]
    highest = lax.Precision.HIGHEST
    blocks = lax.axis_size("rows")
    gathered = lax.all_to_all(bottleneck, "cols", split_axis=0, concat_axis=3, tiled=True)
    samples = gathered.shape[0]
    band = gathered.shape[2] * gathered.shape[3]
    inputs = gathered.reshape(samples, channels, band)
    projected = jnp.einsum(
        "oc,sct->sot", qkv_weight, inputs, preferred_element_type=jnp.float32
    ).astype(jnp.bfloat16)

    def head_scores(query_block, keys_block):
        return (
            jnp.einsum("sdi,sdj->sij", query_block, keys_block, preferred_element_type=jnp.float32)
            * factor
        )

    groups = blocks // heads
    key_count = blocks * band
    quarter = key_count // groups
    position = lax.axis_index("rows")
    part_start = position % groups * quarter
    spread = jnp.broadcast_to(
        projected.reshape(samples, 3, heads, 1, HEAD_DIM, band),
        (samples, 3, heads, groups, HEAD_DIM, band),
    ).reshape(samples, 3, blocks, HEAD_DIM, band)
    headed = lax.all_to_all(spread, "rows", split_axis=2, concat_axis=4, tiled=True)
    head_queries = lax.dynamic_slice_in_dim(headed[:, 0, 0], part_start, quarter, 2)
    head_keys = headed[:, 1, 0]
    head_values = headed[:, 2, 0]

    def head_stats(index, carry):
        top_now, total_now = carry
        scores = head_scores(
            head_queries, lax.dynamic_slice_in_dim(head_keys, index * band, band, 2)
        )
        raised = jnp.maximum(top_now, jnp.max(scores, axis=2))
        total_now = total_now * jnp.exp(top_now - raised) + jnp.sum(
            jnp.exp(scores - raised[..., None]), axis=2
        )
        return (raised, total_now)

    start_top = jnp.full((samples, quarter), -jnp.inf, jnp.float32)
    start_total = jnp.zeros((samples, quarter), jnp.float32)
    head_top, head_total = lax.fori_loop(0, blocks, head_stats, (start_top, start_total))

    def head_output(index, mixed):
        start = index * band
        scores = head_scores(head_queries, lax.dynamic_slice_in_dim(head_keys, start, band, 2))
        attend = (jnp.exp(scores - head_top[..., None]) / head_total[..., None]).astype(
            jnp.bfloat16
        )
        values_block = lax.dynamic_slice_in_dim(head_values, start, band, 2)
        return mixed + jnp.einsum(
            "sij,sdj->sdi", attend, values_block, preferred_element_type=jnp.float32
        )

    head_mixed = lax.fori_loop(
        0, blocks, head_output, jnp.zeros((samples, HEAD_DIM, quarter), jnp.float32)
    ).astype(jnp.bfloat16)
    padded_out = lax.dynamic_update_slice_in_dim(
        jnp.zeros((samples, HEAD_DIM, key_count), jnp.bfloat16), head_mixed, part_start, 2
    )
    returned = lax.all_to_all(
        padded_out.reshape(samples, 1, HEAD_DIM, blocks, band),
        "rows",
        split_axis=3,
        concat_axis=1,
        tiled=True,
    )
    attended = (
        returned.reshape(samples, heads, groups, HEAD_DIM, band)
        .astype(jnp.float32)
        .sum(axis=2)
        .astype(jnp.bfloat16)
    )
    flat = attended.reshape(samples, channels, band)
    branch = jnp.einsum("oc,sct->sot", out_weight, flat, preferred_element_type=jnp.float32)
    updated = (inputs.astype(jnp.float32) + branch).astype(jnp.bfloat16)
    dispersed = lax.all_to_all(
        updated.reshape(gathered.shape), "cols", split_axis=3, concat_axis=0, tiled=True
    )
    onehot = (noise_level[:, None] == jnp.arange(levels, dtype=jnp.int32)[None, :]).astype(
        jnp.float32
    )
    scale_rows = 1.0 + jnp.dot(onehot, film_scale, precision=highest)
    shift_rows = jnp.dot(onehot, film_shift, precision=highest)
    lifted = jnp.einsum("oc,bchw->bohw", up_weight, dispersed, preferred_element_type=jnp.float32)
    lifted = jnp.repeat(jnp.repeat(lifted, 2, axis=2), 2, axis=3)
    summed = lifted + skip_field.astype(jnp.float32)
    active = summed * scale_rows[:, :, None, None] + shift_rows[:, :, None, None]
    sigmoid = jax.nn.sigmoid(active)
    hidden = (active * sigmoid).astype(jnp.bfloat16)
    padded = with_halo(hidden, (("rows", 2), ("cols", 3)), 1)
    grad_pad = with_halo(cotangent, (("rows", 2), ("cols", 3)), 1)
    fine_rows, fine_cols = (hidden.shape[2], hidden.shape[3])
    result = jnp.zeros(hidden.shape, jnp.float32)
    grad_hidden = jnp.zeros(hidden.shape, jnp.float32)
    conv_terms = []
    for number, (row_step, col_step) in enumerate(OFFSETS):
        window = padded[
            :, :, 1 + row_step : 1 + row_step + fine_rows, 1 + col_step : 1 + col_step + fine_cols
        ]
        result = result + jnp.einsum(
            "oc,bchw->bohw", conv_weight[number], window, preferred_element_type=jnp.float32
        )
        shifted = grad_pad[
            :, :, 1 - row_step : 1 - row_step + fine_rows, 1 - col_step : 1 - col_step + fine_cols
        ]
        grad_hidden = grad_hidden + jnp.einsum(
            "oc,bohw->bchw", conv_weight[number], shifted, preferred_element_type=jnp.float32
        )
        conv_terms.append(
            jnp.einsum("bohw,bchw->oc", cotangent, window, preferred_element_type=jnp.float32)
        )
    decoded = result.astype(jnp.bfloat16)
    slope = sigmoid * (1.0 + active * (1.0 - sigmoid))
    grad_active = grad_hidden * slope
    grad_summed = grad_active * scale_rows[:, :, None, None]
    scale_terms = jnp.sum(grad_active * summed, axis=(2, 3))
    shift_terms = jnp.sum(grad_active, axis=(2, 3))
    grad_skip = grad_summed.astype(jnp.bfloat16)
    coarse = (
        grad_summed.reshape(batch, narrow, tile_rows, 2, tile_cols, 2)
        .sum(axis=(3, 5))
        .astype(jnp.bfloat16)
    )
    up_term = jnp.einsum("bohw,bchw->oc", coarse, dispersed, preferred_element_type=jnp.float32)
    grad_lifted = jnp.einsum("oc,bohw->bchw", up_weight, coarse, preferred_element_type=jnp.float32)
    scale_term = jnp.dot(onehot.T, scale_terms, precision=highest)
    shift_term = jnp.dot(onehot.T, shift_terms, precision=highest)
    conv_sum, up_sum, scale_sum, shift_sum = packed_total(
        (jnp.stack(conv_terms), up_term, scale_term, shift_term), ("rows", "cols")
    )
    grad_band = lax.all_to_all(
        grad_lifted, "cols", split_axis=0, concat_axis=3, tiled=True
    ).reshape(samples, channels, band)
    grad_low = grad_band.astype(jnp.bfloat16)
    out_term = jnp.einsum("sct,sdt->cd", grad_low, flat, preferred_element_type=jnp.float32)
    grad_attended = jnp.einsum(
        "cd,sct->sdt", out_weight, grad_low, preferred_element_type=jnp.float32
    ).astype(jnp.bfloat16)
    grad_attended = grad_attended.reshape(samples, heads, HEAD_DIM, band)
    grad_spread = jnp.broadcast_to(
        grad_attended.reshape(samples, heads, 1, HEAD_DIM, band),
        (samples, heads, groups, HEAD_DIM, band),
    ).reshape(samples, blocks, HEAD_DIM, band)
    grad_headed = lax.all_to_all(grad_spread, "rows", split_axis=1, concat_axis=3, tiled=True)
    head_grads = lax.dynamic_slice_in_dim(grad_headed[:, 0], part_start, quarter, 2)
    head_deltas = jnp.sum(head_grads.astype(jnp.float32) * head_mixed.astype(jnp.float32), axis=1)

    def head_back(index, carry):
        query_grad, key_buffer, value_buffer = carry
        start = index * band
        keys_block = lax.dynamic_slice_in_dim(head_keys, start, band, 2)
        values_block = lax.dynamic_slice_in_dim(head_values, start, band, 2)
        scores = head_scores(head_queries, keys_block)
        probs = jnp.exp(scores - head_top[..., None]) / head_total[..., None]
        dots = jnp.einsum(
            "sdi,sdj->sij", head_grads, values_block, preferred_element_type=jnp.float32
        )
        score_grad = (probs * (dots - head_deltas[..., None])).astype(jnp.bfloat16)
        value_part = jnp.einsum(
            "sij,sdi->sdj",
            probs.astype(jnp.bfloat16),
            head_grads,
            preferred_element_type=jnp.float32,
        )
        query_grad = (
            query_grad
            + jnp.einsum("sij,sdj->sdi", score_grad, keys_block, preferred_element_type=jnp.float32)
            * factor
        )
        key_part = (
            jnp.einsum("sij,sdi->sdj", score_grad, head_queries, preferred_element_type=jnp.float32)
            * factor
        )
        key_buffer = lax.dynamic_update_slice_in_dim(key_buffer, key_part, start, 2)
        value_buffer = lax.dynamic_update_slice_in_dim(value_buffer, value_part, start, 2)
        return (query_grad, key_buffer, value_buffer)

    whole = jnp.zeros((samples, HEAD_DIM, key_count), jnp.float32)
    start_query = jnp.zeros((samples, HEAD_DIM, quarter), jnp.float32)
    head_query_grad, key_buffer, value_buffer = lax.fori_loop(
        0, blocks, head_back, (start_query, whole, whole)
    )
    query_buffer = lax.dynamic_update_slice_in_dim(whole, head_query_grad, part_start, 2)
    partial_value = jnp.stack([query_buffer, key_buffer, value_buffer], axis=1).reshape(
        samples, 3, 1, HEAD_DIM, blocks, band
    )
    collected = lax.all_to_all(partial_value, "rows", split_axis=4, concat_axis=2, tiled=True)
    stacked = (
        collected.reshape(samples, 3, heads, groups, HEAD_DIM, band)
        .sum(axis=3)
        .reshape(samples, 3 * channels, band)
        .astype(jnp.bfloat16)
    )
    qkv_term = jnp.einsum("sot,sct->oc", stacked, inputs, preferred_element_type=jnp.float32)
    grad_inputs = grad_band + jnp.einsum(
        "oc,sot->sct", qkv_weight, stacked, preferred_element_type=jnp.float32
    )
    grad_bottleneck = lax.all_to_all(
        grad_inputs.reshape(gathered.shape), "cols", split_axis=3, concat_axis=0, tiled=True
    )
    qkv_sum, out_sum = packed_total((qkv_term, out_term), ("rows", "cols"))
    return (
        decoded,
        grad_bottleneck,
        grad_skip,
        qkv_sum,
        out_sum,
        up_sum,
        conv_sum,
        scale_sum,
        shift_sum,
    )


def solution(mesh):
    in_specs = (
        P(None, None, "rows", "cols"),
        P(None, None, "rows", "cols"),
        P(None, None, "rows", "cols"),
        P(),
        P(),
        P(),
        P(),
        P(),
        P(),
        P(),
    )
    out_specs = (
        P(None, None, "rows", "cols"),
        P(None, None, "rows", "cols"),
        P(None, None, "rows", "cols"),
        P(),
        P(),
        P(),
        P(),
        P(),
        P(),
    )
    return jax.shard_map(
        on_device, mesh=mesh, in_specs=in_specs, out_specs=out_specs, check_vma=False
    )
```

profile of v0, /device:TPU:1, one launch (start us, length us, event | category | flops | bytes accessed | tf_op | source)
XLA Modules:
  0.0 486.1 jit_solution(9553448003747211766)
XLA Ops:
  7.2 6.5 %all-to-all-start = ((bf16[8,256,1,32]{1,3,2,0:T(8,128)(2,1)}), bf16[8,256,1,32]{1,3,2,0:T(8,128)(2,1)S(1)}, u32[]{:S(2)}, u32[]{:S(2)}) async-start(bf16[8,256,1,32]{1,3,2,0:T(8,128)(2,1)} %param.16), calls=%async_computation | async-start | bytes 262144 | tf_op jit(solution)/shard_map/all_to_all | solution.py:59
  14.7 6.1 %collective-permute-start.4 = (bf16[8,128,1,64]{1,3,2,0:T(8,128)(2,1)S(1)}, bf16[8,128,1,64]{1,3,2,0:T(8,128)(2,1)S(1)}, u32[]{:S(2)}, u32[]{:S(2)}) collective-permute-start(bf16[8,128,1,64]{1,3,2,0:T(8,128)(2,1)S(1)} %get-tuple-element.567), channel_id=1, source_target_pairs={{0,8},{8,16},{16,24},{24,32},{32,40},{40,48},{48,56},{56,64},{64,7... | collective-permute-start | bytes 393224 | tf_op jit(solution)/shard_map/ppermute | solution.py:22
  20.8 1.9 collective-permute-start.5
  27.4 7.5 %all-to-all-start.1 = ((bf16[1,3,16,64,256]{4,3,1,0,2:T(8,128)(2,1)}), bf16[1,3,16,64,256]{4,3,1,0,2:T(8,128)(2,1)}, u32[]{:S(2)}, u32[]{:S(2)}) async-start(bf16[1,3,16,64,256]{4,3,1,0,2:T(8,128)(2,1)} %bitcast.8), calls=%async_computation.1 | async-start | bytes 3145728 | tf_op jit(solution)/shard_map/all_to_all | solution.py:82
  35.7 3.0 collective-permute-start.7
  47.1 10.6 %all-to-all-done.1 = bf16[1,3,16,64,256]{4,3,1,0,2:T(8,128)(2,1)} async-done(((bf16[1,3,16,64,256]{4,3,1,0,2:T(8,128)(2,1)}), bf16[1,3,16,64,256]{4,3,1,0,2:T(8,128)(2,1)}, u32[]{:S(2)}, u32[]{:S(2)}) %all-to-all-start.1) | async-done | bytes 1572896 | tf_op jit(solution)/shard_map/all_to_all | solution.py:82
  60.4 21.6 %while.48 = (s32[]{:T(128)}, f32[1,1024]{1,0:T(1,128)S(1)}, f32[1,1024]{1,0:T(1,128)S(1)}, bf16[1,64,4096]{2,1,0:T(8,128)(2,1)}, bf16[1,64,1024]{2,1,0:T(8,128)(...) while((s32[]{:T(128)}, f32[1,1024]{1,0:T(1,128)S(1)}, f32[1,1024]{1,0:T(1,128)S(1)}, ...), condition=%wide.region_3.4_spmd.clone, body=%wide.region_0.3_spmd.clone.sunk | while | flops 34608132 | bytes 2314402 | solution.py:100
  82.0 21.6 %while.49 = (s32[]{:T(128)}, f32[1,64,1024]{2,1,0:T(8,128)S(1)}, bf16[1,64,4096]{2,1,0:T(8,128)(2,1)}, bf16[1,64,4096]{2,1,0:T(8,128)(2,1)}, bf16[1,64,1024]{2,1...) while((s32[]{:T(128)}, f32[1,64,1024]{2,1,0:T(8,128)S(1)}, ...), condition=%wide.region_5.6_spmd.clone, body=%wide.region_4.5_spmd.clone.sunk | while | flops 68288520 | bytes 730796 | solution.py:113
  104.8 6.4 %all-to-all-start.2 = ((bf16[1,1,64,16,256]{4,2,1,0,3:T(8,128)(2,1)}), bf16[1,1,64,16,256]{4,2,1,0,3:T(8,128)(2,1)}, u32[]{:S(2)}, u32[]{:S(2)}) async-start(bf16[1,1,64,16,256]{4,2,1,0,3:T(8,128)(2,1)} %copy.40), calls=%async_computation.2 | async-start | bytes 1048576 | tf_op jit(solution)/shard_map/all_to_all | solution.py:119
  112.2 1.9 fusion.60
  114.1 8.4 %all-to-all-done.2 = bf16[1,1,64,16,256]{4,2,1,0,3:T(8,128)(2,1)} async-done(((bf16[1,1,64,16,256]{4,2,1,0,3:T(8,128)(2,1)}), bf16[1,1,64,16,256]{4,2,1,0,3:T(8,128)(2,1)}, u32[]{:S(2)}, u32[]{:S(2)}) %all-to-all-start.2) | async-done | bytes 524320 | tf_op jit(solution)/shard_map/all_to_all | solution.py:119
  126.8 5.8 %all-to-all-start.3 = ((bf16[8,2,4096]{2,1,0:T(2,128)(2,1)}), bf16[8,2,4096]{2,1,0:T(2,128)(2,1)S(1)}, u32[]{:S(2)}, u32[]{:S(2)}) async-start(bf16[8,2,4096]{2,1,0:T(2,128)(2,1)} %reshape.403), calls=%async_computation.3 | async-start | bytes 262144 | tf_op jit(solution)/shard_map/all_to_all | solution.py:135
  134.4 3.4 all-to-all-done.3
  138.3 2.7 multiply_reduce_fusion
  143.3 4.6 collective-permute-start.1
  147.9 2.5 collective-permute-start
  150.4 3.4 all-to-all-start.4
  156.4 3.3 collective-permute-start.2
  172.9 5.1 %all-to-all-start.5 = ((bf16[1,16,64,256]{3,2,0,1:T(8,128)(2,1)}), bf16[1,16,64,256]{3,2,0,1:T(8,128)(2,1)S(1)}, u32[]{:S(2)}, u32[]{:S(2)}) async-start(bf16[1,16,64,256]{3,2,0,1:T(8,128)(2,1)} %bitcast.87), calls=%async_computation.5 | async-start | bytes 1048576 | tf_op jit(solution)/shard_map/all_to_all | solution.py:203
  178.9 2.1 copy.53
  181.0 1.8 fusion.108
  182.8 1.8 fusion.111
  184.6 4.6 all-to-all-done.5
  191.0 70.9 %while.50 = (s32[]{:T(128)}, f32[1,64,1024]{2,1,0:T(8,128)S(1)}, f32[1,64,4096]{2,1,0:T(8,128)S(1)}, f32[1,64,4096]{2,1,0:T(8,128)}, bf16[1,64,4096]{2,1,0:T(8,1...) while((s32[]{:T(128)}, f32[1,64,1024]{2,1,0:T(8,128)S(1)}, ...), condition=%wide.region_11.12_spmd.clone, body=%wide.region_10.11_spmd.clone.sunk | while | flops 169820160 | bytes 6009057 | solution.py:239
  264.5 3.5 copy.48
  268.0 4.9 %all-to-all-start.6 = ((f32[1,3,1,64,16,256]{5,3,2,1,0,4:T(8,128)}), f32[1,3,1,64,16,256]{5,3,2,1,0,4:T(8,128)S(1)}, u32[]{:S(2)}, u32[]{:S(2)}) async-start(f32[1,3,1,64,16,256]{5,3,2,1,0,4:T(8,128)} %copy.48), calls=%async_computation.6 | async-start | bytes 6291456 | tf_op jit(solution)/shard_map/all_to_all | solution.py:246
  273.0 2.0 fusion.116
  275.0 1.8 pad_maximum_fusion.2
  277.9 34.6 %all-to-all-done.6 = f32[1,3,1,64,16,256]{5,3,2,1,0,4:T(8,128)S(1)} async-done(((f32[1,3,1,64,16,256]{5,3,2,1,0,4:T(8,128)}), f32[1,3,1,64,16,256]{5,3,2,1,0,4:T(8,128)S(1)}, u32[]{:S(2)}, u32[]{:S(2)}) %all-to-all-start.6) | async-done | bytes 3145760 | tf_op jit(solution)/shard_map/all_to_all | solution.py:246
  322.0 5.5 %all-to-all-start.7 = ((f32[1,256,1,256]{1,2,0,3:T(1,128)}), f32[1,256,1,256]{1,2,0,3:T(1,128)S(1)}, u32[]{:S(2)}, u32[]{:S(2)}) async-start(f32[1,256,1,256]{1,2,0,3:T(1,128)} %copy.51), calls=%async_computation.7 | async-start | bytes 524288 | tf_op jit(solution)/shard_map/all_to_all | solution.py:257
  329.2 4.0 all-to-all-done.7
  334.0 139.0 %all-reduce.3.cloned.1.call-done = (f32[262144]{0:T(1024)}, f32[184832]{0:T(1024)}) async-done(((f32[262144]{0:T(1024)}, f32[184832]{0:T(1024)}), (f32[262144]{0:T(1024)}, f32[184832]{0:T(1024)})) %all-reduce.3.cloned.1.call-update) | async-done | bytes 1787920 | tf_op jit(solution)/shard_map/psum | solution.py:33
  (359 shorter events, 180.7 us)
Async XLA Ops:
  7.2 18.4 %copy-start = (bf16[768,256]{1,0:T(8,128)(2,1)S(1)}, bf16[768,256]{1,0:T(8,128)(2,1)}, u32[]{:S(2)}) copy-start(bf16[768,256]{1,0:T(8,128)(2,1)} %param.20) | copy-start | bytes 1179652
  7.2 16.8 %copy-start.32 = (f32[18,128]{1,0:T(8,128)S(1)}, f32[18,128]{1,0:T(8,128)}, u32[]{:S(2)}) copy-start(f32[18,128]{1,0:T(8,128)} %param.24) | copy-start | bytes 27652
  7.2 16.8 %copy-start.34 = (s32[8]{0:T(128)S(1)}, s32[8]{0:T(128)}, u32[]{:S(2)}) copy-start(s32[8]{0:T(128)} %param.19) | copy-start | bytes 100
  7.2 17.5 %copy-start.33 = (f32[18,128]{1,0:T(8,128)S(1)}, f32[18,128]{1,0:T(8,128)}, u32[]{:S(2)}) copy-start(f32[18,128]{1,0:T(8,128)} %param.25) | copy-start | bytes 27652
  7.2 18.3 %all-to-all-start = ((bf16[8,256,1,32]{1,3,2,0:T(8,128)(2,1)}), bf16[8,256,1,32]{1,3,2,0:T(8,128)(2,1)S(1)}, u32[]{:S(2)}, u32[]{:S(2)}) async-start(bf16[8,256,1,32]{1,3,2,0:T(8,128)(2,1)} %param.16), calls=%async_computation | async-start | bytes 262144 | tf_op jit(solution)/shard_map/all_to_all | solution.py:59
  14.7 20.2 %collective-permute-start.4 = (bf16[8,128,1,64]{1,3,2,0:T(8,128)(2,1)S(1)}, bf16[8,128,1,64]{1,3,2,0:T(8,128)(2,1)S(1)}, u32[]{:S(2)}, u32[]{:S(2)}) collective-permute-start(bf16[8,128,1,64]{1,3,2,0:T(8,128)(2,1)S(1)} %get-tuple-element.567), channel_id=1, source_target_pairs={{0,8},{8,16},{16,24},{24,32},{32,40},{40,48},{48,56},{56,64},{64,7... | collective-permute-start | bytes 393224 | tf_op jit(solution)/shard_map/ppermute | solution.py:22
  20.8 14.2 %collective-permute-start.5 = (bf16[8,128,1,64]{1,3,2,0:T(8,128)(2,1)S(1)}, bf16[8,128,1,64]{1,3,2,0:T(8,128)(2,1)S(1)}, u32[]{:S(2)}, u32[]{:S(2)}) collective-permute-start(bf16[8,128,1,64]{1,3,2,0:T(8,128)(2,1)S(1)} %get-tuple-element.566), channel_id=1, source_target_pairs={{8,0},{16,8},{24,16},{32,24},{40,32},{48,40},{56,48},{64,56},{72,6... | collective-permute-start | bytes 393224 | tf_op jit(solution)/shard_map/ppermute | solution.py:24
  25.5 98.1 %copy-start.10 = (bf16[8,256,1,32]{1,3,2,0:T(8,128)(2,1)}, bf16[8,256,1,32]{1,3,2,0:T(8,128)(2,1)S(1)}, u32[]{:S(2)}) copy-start(bf16[8,256,1,32]{1,3,2,0:T(8,128)(2,1)S(1)} %all-to-all-done) | copy-start | bytes 393220
  27.4 7.5 %copy-start.1 = (bf16[8,128,2,64]{1,3,2,0:T(8,128)(2,1)S(1)}, bf16[8,128,2,64]{1,3,2,0:T(8,128)(2,1)}, u32[]{:S(2)}) copy-start(bf16[8,128,2,64]{1,3,2,0:T(8,128)(2,1)} %param.18) | copy-start | bytes 786436
  27.4 30.3 %all-to-all-start.1 = ((bf16[1,3,16,64,256]{4,3,1,0,2:T(8,128)(2,1)}), bf16[1,3,16,64,256]{4,3,1,0,2:T(8,128)(2,1)}, u32[]{:S(2)}, u32[]{:S(2)}) async-start(bf16[1,3,16,64,256]{4,3,1,0,2:T(8,128)(2,1)} %bitcast.8), calls=%async_computation.1 | async-start | bytes 3145728 | tf_op jit(solution)/shard_map/all_to_all | solution.py:82
  35.7 7.9 %collective-permute-start.7 = (bf16[8,128,4,1]{1,3,2,0:T(2,128)(2,1)S(1)}, bf16[8,128,4,1]{1,3,2,0:T(2,128)(2,1)S(1)}, u32[]{:S(2)}, u32[]{:S(2)}) collective-permute-start(bf16[8,128,4,1]{1,3,2,0:T(2,128)(2,1)S(1)} %get-tuple-element.561), channel_id=1, source_target_pairs={{0,1},{1,2},{2,3},{3,4},{4,5},{5,6},{6,7},{8,9},{9,10},{10,11},{11... | collective-permute-start | bytes 24584 | tf_op jit(solution)/shard_map/ppermute | solution.py:22
  38.7 72.5 %collective-permute-start.6 = (bf16[8,128,4,1]{1,3,2,0:T(2,128)(2,1)}, bf16[8,128,4,1]{1,3,2,0:T(2,128)(2,1)}, u32[]{:S(2)}, u32[]{:S(2)}) collective-permute-start(bf16[8,128,4,1]{1,3,2,0:T(2,128)(2,1)} %get-tuple-element.560), channel_id=1, source_target_pairs={{1,0},{2,1},{3,2},{4,3},{5,4},{6,5},{7,6},{9,8},{10,9},{11,10},{12... | collective-permute-start | bytes 24584 | tf_op jit(solution)/shard_map/ppermute | solution.py:24
  43.6 15.8 %copy-start.29 = (bf16[8,128,4,1]{1,3,2,0:T(2,128)(2,1)}, bf16[8,128,4,1]{1,3,2,0:T(2,128)(2,1)S(1)}, u32[]{:S(2)}) copy-start(bf16[8,128,4,1]{1,3,2,0:T(2,128)(2,1)S(1)} %collective-permute-done.7) | copy-start | bytes 24580
  104.8 7.4 %copy-start.8 = (f32[8,2,64,128]{3,2,1,0:T(8,128)S(1)}, f32[8,2,64,128]{3,2,1,0:T(8,128)}, u32[]{:S(2)}) copy-start(f32[8,2,64,128]{3,2,1,0:T(8,128)} %fusion.83) | copy-start | bytes 1572868
  104.8 7.4 %copy-start.9 = (f32[8,2,64,128]{3,2,1,0:T(8,128)S(1)}, f32[8,2,64,128]{3,2,1,0:T(8,128)}, u32[]{:S(2)}) copy-start(f32[8,2,64,128]{3,2,1,0:T(8,128)} %fusion.94) | copy-start | bytes 1572868
  104.8 17.7 %all-to-all-start.2 = ((bf16[1,1,64,16,256]{4,2,1,0,3:T(8,128)(2,1)}), bf16[1,1,64,16,256]{4,2,1,0,3:T(8,128)(2,1)}, u32[]{:S(2)}, u32[]{:S(2)}) async-start(bf16[1,1,64,16,256]{4,2,1,0,3:T(8,128)(2,1)} %copy.40), calls=%async_computation.2 | async-start | bytes 1048576 | tf_op jit(solution)/shard_map/all_to_all | solution.py:119
  112.2 11.5 %copy-start.27 = (bf16[256,256]{1,0:T(8,128)(2,1)S(1)}, bf16[256,256]{1,0:T(8,128)(2,1)}, u32[]{:S(2)}) copy-start(bf16[256,256]{1,0:T(8,128)(2,1)} %param.21) | copy-start | bytes 393220
  122.5 10.1 %copy-start.21 = (bf16[9,128,128]{2,1,0:T(8,128)(2,1)S(1)}, bf16[9,128,128]{2,1,0:T(8,128)(2,1)}, u32[]{:S(2)}) copy-start(bf16[9,128,128]{2,1,0:T(8,128)(2,1)} %param.23) | copy-start | bytes 884740
  123.7 10.7 %copy-start.19 = (bf16[4,64,256]{2,1,0:T(8,128)(2,1)}, bf16[4,64,256]{2,1,0:T(8,128)(2,1)S(1)}, u32[]{:S(2)}) copy-start(bf16[4,64,256]{2,1,0:T(8,128)(2,1)S(1)} %reduce_sum.79) | copy-start | bytes 393220
  126.1 11.9 %copy-start.28 = (bf16[128,256]{1,0:T(8,128)(2,1)S(1)}, bf16[128,256]{1,0:T(8,128)(2,1)}, u32[]{:S(2)}) copy-start(bf16[128,256]{1,0:T(8,128)(2,1)} %param.22) | copy-start | bytes 196612
  126.8 11.0 %all-to-all-start.3 = ((bf16[8,2,4096]{2,1,0:T(2,128)(2,1)}), bf16[8,2,4096]{2,1,0:T(2,128)(2,1)S(1)}, u32[]{:S(2)}, u32[]{:S(2)}) async-start(bf16[8,2,4096]{2,1,0:T(2,128)(2,1)} %reshape.403), calls=%async_computation.3 | async-start | bytes 262144 | tf_op jit(solution)/shard_map/all_to_all | solution.py:135
  143.3 13.0 %collective-permute-start.1 = (bf16[8,128,1,64]{1,3,2,0:T(8,128)(2,1)S(1)}, bf16[8,128,1,64]{1,3,2,0:T(8,128)(2,1)S(1)}, u32[]{:S(2)}, u32[]{:S(2)}) collective-permute-start(bf16[8,128,1,64]{1,3,2,0:T(8,128)(2,1)S(1)} %get-tuple-element.569), channel_id=1, source_target_pairs={{8,0},{16,8},{24,16},{32,24},{40,32},{48,40},{56,48},{64,56},{72,6... | collective-permute-start | bytes 393224 | tf_op jit(solution)/shard_map/ppermute | solution.py:24
  147.9 8.5 %collective-permute-start = (bf16[8,128,1,64]{1,3,2,0:T(8,128)(2,1)S(1)}, bf16[8,128,1,64]{1,3,2,0:T(8,128)(2,1)S(1)}, u32[]{:S(2)}, u32[]{:S(2)}) collective-permute-start(bf16[8,128,1,64]{1,3,2,0:T(8,128)(2,1)S(1)} %get-tuple-element.568), channel_id=1, source_target_pairs={{0,8},{8,16},{16,24},{24,32},{32,40},{40,48},{48,56},{56,64},{64,7... | collective-permute-start | bytes 393224 | tf_op jit(solution)/shard_map/ppermute | solution.py:22
  150.4 21.3 %all-to-all-start.4 = ((f32[8,256,1,32]{1,3,2,0:T(8,128)}), f32[8,256,1,32]{1,3,2,0:T(8,128)S(1)}, u32[]{:S(2)}, u32[]{:S(2)}) async-start(f32[8,256,1,32]{1,3,2,0:T(8,128)} %convolution_bitcast_fusion.4), calls=%async_computation.4 | async-start | bytes 524288 | tf_op jit(solution)/shard_map/all_to_all | solution.py:190
  156.4 6.6 %collective-permute-start.2 = (bf16[8,128,4,1]{1,3,2,0:T(2,128)(2,1)S(1)}, bf16[8,128,4,1]{1,3,2,0:T(2,128)(2,1)S(1)}, u32[]{:S(2)}, u32[]{:S(2)}) collective-permute-start(bf16[8,128,4,1]{1,3,2,0:T(2,128)(2,1)S(1)} %get-tuple-element.564), channel_id=1, source_target_pairs={{0,1},{1,2},{2,3},{3,4},{4,5},{5,6},{6,7},{8,9},{9,10},{10,11},{11... | collective-permute-start | bytes 24584 | tf_op jit(solution)/shard_map/ppermute | solution.py:22
  159.6 4.5 collective-permute-start.3
  164.4 16.6 %copy-start.3 = (bf16[8,128,4,65]{1,3,2,0:T(8,128)(2,1)}, bf16[8,128,4,65]{1,3,2,0:T(8,128)(2,1)S(1)}, u32[]{:S(2)}) copy-start(bf16[8,128,4,65]{1,3,2,0:T(8,128)(2,1)S(1)} %get-tuple-element.563) | copy-start | bytes 1597444
  164.5 18.4 %copy-start.2 = (bf16[8,128,4,65]{1,3,2,0:T(8,128)(2,1)}, bf16[8,128,4,65]{1,3,2,0:T(8,128)(2,1)S(1)}, u32[]{:S(2)}) copy-start(bf16[8,128,4,65]{1,3,2,0:T(8,128)(2,1)S(1)} %get-tuple-element.562) | copy-start | bytes 1597444
  172.9 16.3 %all-to-all-start.5 = ((bf16[1,16,64,256]{3,2,0,1:T(8,128)(2,1)}), bf16[1,16,64,256]{3,2,0,1:T(8,128)(2,1)S(1)}, u32[]{:S(2)}, u32[]{:S(2)}) async-start(bf16[1,16,64,256]{3,2,0,1:T(8,128)(2,1)} %bitcast.87), calls=%async_computation.5 | async-start | bytes 1048576 | tf_op jit(solution)/shard_map/all_to_all | solution.py:203
  268.0 44.5 %all-to-all-start.6 = ((f32[1,3,1,64,16,256]{5,3,2,1,0,4:T(8,128)}), f32[1,3,1,64,16,256]{5,3,2,1,0,4:T(8,128)S(1)}, u32[]{:S(2)}, u32[]{:S(2)}) async-start(f32[1,3,1,64,16,256]{5,3,2,1,0,4:T(8,128)} %copy.48), calls=%async_computation.6 | async-start | bytes 6291456 | tf_op jit(solution)/shard_map/all_to_all | solution.py:246
  272.9 200.1 %all-reduce.3.cloned.1.call-start = ((), (), s32[]{:S(2)}) async-start(), calls=%async_computation.8 | async-start | bytes 3579904 | tf_op jit(solution)/shard_map/psum | solution.py:33
  322.0 11.2 %all-to-all-start.7 = ((f32[1,256,1,256]{1,2,0,3:T(1,128)}), f32[1,256,1,256]{1,2,0,3:T(1,128)S(1)}, u32[]{:S(2)}, u32[]{:S(2)}) async-start(f32[1,256,1,256]{1,2,0,3:T(1,128)} %copy.51), calls=%async_computation.7 | async-start | bytes 524288 | tf_op jit(solution)/shard_map/all_to_all | solution.py:257
  (22 other events, 86.9 us)
Sparse Core Ops, SparseCore 0:
  317.5 155.4 all-reduce.2
where the time goes:
time: 494 us; the launch traced here: 486 us
  waiting for transfers between devices  206 us (42%)
  matrix products  153 us (31%)
  starting transfers between devices  69.1 us (14%)
  local copies, waits for them, and re-layouts  31.3 us (6%)
  between operations  14.9 us (3%)
  other arithmetic  10.7 us (2%)
    psum x1, waiting for transfers between devices, packed_total(): so_far = lax.psum(flat, axis)  139 us
    dot_general x32, matrix products, head_scores(): jnp.einsum('sdi,sdj->sij', query_block, keys_block, preferred_element_typ...  35.3 us
    all_to_all x1, waiting for transfers between devices, on_device(): lax.all_to_all(partial_value, 'rows', split_axis=4, concat_axis=2, tiled=...  34.6 us
    dot_general x16, matrix products, head_output(): jnp.einsum('sij,sdj->sdi', attend, values_block, preferred_element_type=j...  21.1 us
    dot_general x16, matrix products, head_back(): jnp.einsum('sdi,sdj->sij', head_grads, values_block, preferred_element_ty...  17.3 us
    dot_general x16, matrix products, head_back(): jnp.einsum('sij,sdj->sdi', score_grad, keys_block, preferred_element_type...  15.8 us
    dot_general x9, matrix products, on_device(): jnp.einsum('oc,bohw->bchw', conv_weight[number], shifted, preferred_eleme...  15.6 us
    dot_general x16, matrix products, head_back(): jnp.einsum('sij,sdi->sdj', probs.astype(jnp.bfloat16), head_grads, prefer...  14.9 us
  transfers between devices with their start and end apart: 17, of which 8 were waited for; matrix products, arithmetic and copies ran while one was open for 19% of the time, Pallas kernels for 0%

commit v1 on v0

v1 whole, which is shorter than its diff:
```python
import functools

import jax
import jax.numpy as jnp
from jax import lax
from jax.experimental import pallas as pl
from jax.experimental.pallas import tpu as pltpu
from jax.sharding import PartitionSpec as P

MESH = pl.DeviceIdType.MESH
BF = jnp.bfloat16
F32 = jnp.float32
ROWS, COLS = 16, 8
HEADS = 4
BLOCK = 256
CHUNK = 1024
TAPS = [(-1, -1), (-1, 0), (-1, 1), (0, -1), (0, 0), (0, 1), (1, -1), (1, 0), (1, 1)]
VMEM = pl.BlockSpec(memory_space=pltpu.VMEM)


def nn(a, b):
    return lax.dot_general(a, b, (((1,), (0,)), ((), ())), preferred_element_type=F32)


def nt(a, b):
    return lax.dot_general(a, b, (((1,), (1,)), ((), ())), preferred_element_type=F32)


def remote(src, dst, send, recv, row, col):
    return pltpu.make_async_remote_copy(
        src_ref=src, dst_ref=dst, send_sem=send, recv_sem=recv, device_id=(row, col), device_id_type=MESH
    )


def send_or_keep(here, src, dst, send, recv, row, col):
    @pl.when(here)
    def _():
        pltpu.make_async_copy(src, dst, recv).start()

    @pl.when(jnp.logical_not(here))
    def _():
        remote(src, dst, send, recv, row, col).start()


def drain(ref, sem):
    pltpu.make_async_copy(ref, ref, sem).wait()


def loop(lo, hi, body):
    def step(i, carry):
        body(i)
        return carry

    lax.fori_loop(lo, hi, step, 0)


def kernel(
    x_ref, skip_ref, cot_ref, noise_col, noise_row, wqkv, woutn, wup, wconv, fscale, fshift,
    dec_ref, gb_ref, gskip_ref, gqkv_ref, gout_ref, gup_ref, gconv_ref, gscale_ref, gshift_ref,
    wq, wkv, kv_send, q_send, kv_in, q_in, v1, s_ref, p_ref, invl_ref, o_buf, ocell,
    gx, hx, gt, gedge, hedge, ghalo, hhalo, pre_ref, act_ref, dh_ref, y_ref, dy_ref, du_ref,
    do_send, do_in, dkvt, dq_buf, dq_in, pair_send, pair_in, dkv_send, dkv_in, gacc,
    eg, epin, ehs, ersin, eag, lg, lpin, lhs, lrsin, lag, sems,
):
    r, c = lax.axis_index("rows"), lax.axis_index("cols")
    me = r * COLS + c
    par = lax.rem(r, 2)
    mate = r + 1 - 2 * par
    kslot = lax.div(r, 2) * COLS + c
    head, quarter = lax.div(r, 4), lax.rem(r, 4)
    qslot = quarter * COLS + c
    own = head == quarter
    pair_index = c * HEADS + head

    barrier = pltpu.get_barrier_semaphore()

    def signal(i):
        d = lax.rem(me + i, ROWS * COLS)
        pl.semaphore_signal(
            barrier, inc=1, device_id=(lax.div(d, COLS), lax.rem(d, COLS)), device_id_type=MESH
        )

    loop(1, ROWS * COLS, signal)

    def to_attention(src, dst, send, recv):
        def one(i):
            k = lax.rem(head * COLS + c + i, 32)
            h, dc = lax.div(k, COLS), lax.rem(k, COLS)
            dr = 4 * h + head
            here = (dr == r) & (dc == c)
            send_or_keep(here, src.at[dc * HEADS + h], dst.at[qslot], send, recv, dr, dc)

        loop(0, 32, one)

    def to_cells(src, dst, send, recv, row):
        def one(i):
            dc = lax.rem(c + i, COLS)
            dr = 4 * quarter + row
            here = (dr == r) & (dc == c)
            send_or_keep(here, src.at[row * COLS + dc], dst.at[pair_index], send, recv, dr, dc)

        loop(0, COLS, one)

    def drain32(ref, sem):
        @pl.when(own)
        def _():
            drain(ref.at[pl.ds(0, 31)], sem)

        @pl.when(jnp.logical_not(own))
        def _():
            drain(ref, sem)

    def parity_device(k):
        return 2 * lax.div(k, COLS) + par, lax.rem(k, COLS)

    def halo_start(ext, edge, halo, base):
        up, down = lax.rem(r + ROWS - 1, ROWS), lax.rem(r + 1, ROWS)
        left, right = lax.rem(c + COLS - 1, COLS), lax.rem(c + 1, COLS)
        copies = [
            remote(ext.at[:, 1, pl.ds(1, 2)], ext.at[:, 3, pl.ds(1, 2)], sems.at[base], sems.at[base + 1], up, c),
            remote(ext.at[:, 2, pl.ds(1, 2)], ext.at[:, 0, pl.ds(1, 2)], sems.at[base + 2], sems.at[base + 3], down, c),
        ]
        at = base + 4
        for row, slot in ((up, 2), (r, 1), (down, 0)):
            copies.append(remote(edge.at[0], halo.at[1, slot], sems.at[at], sems.at[at + 1], row, left))
            copies.append(remote(edge.at[1], halo.at[0, slot], sems.at[at + 2], sems.at[at + 3], row, right))
            at += 4
        for copy in copies:
            copy.start()
        return copies

    def halo_finish(ext, halo, copies):
        for copy in copies:
            copy.wait()

        @pl.when(r == 0)
        def _():
            ext[:, 0, 1:3] = jnp.zeros((8, 2, 32, 128), BF)
            halo[:, 0] = jnp.zeros((2, 2, 8, 128), F32)

        @pl.when(r == ROWS - 1)
        def _():
            ext[:, 3, 1:3] = jnp.zeros((8, 2, 32, 128), BF)
            halo[:, 2] = jnp.zeros((2, 2, 8, 128), F32)

        @pl.when(c == 0)
        def _():
            halo[0] = jnp.zeros((3, 2, 8, 128), F32)

        @pl.when(c == COLS - 1)
        def _():
            halo[1] = jnp.zeros((3, 2, 8, 128), F32)

        place = lax.broadcasted_iota(jnp.int32, (32, 128), 0)

        def one(s):
            for row, (slot, a) in enumerate(((0, 1), (1, 0), (1, 1), (2, 0))):
                odd = ext[s, row, 2].astype(F32)
                even = ext[s, row, 1].astype(F32)
                before = halo[0, slot, a, pl.ds(s, 1), :]
                after = halo[1, slot, a, pl.ds(s, 1), :]
                ext[s, row, 0] = jnp.where(place == 0, before, pltpu.roll(odd, 1, axis=0)).astype(BF)
                ext[s, row, 3] = jnp.where(place == 31, after, pltpu.roll(even, 31, axis=0)).astype(BF)

        loop(0, 8, one)

    class Total:
        def __init__(self, count, g, pin, hs, rsin, ag, base):
            self.count, self.g, self.pin, self.hs, self.rsin, self.ag = count, g, pin, hs, rsin, ag
            self.sem = [sems.at[base + i] for i in range(8)]
            self.reducer = kslot < count

        def start(self):
            remote(self.g.at[1 - par], self.pin, self.sem[0], self.sem[1], mate, c).start()

        def scatter(self):
            remote(self.g.at[1 - par], self.pin, self.sem[0], self.sem[1], mate, c).wait()
            self.hs[...] = (self.g[par].astype(F32) + self.pin[...].astype(F32)).astype(BF)

            def one(i):
                k = lax.rem(kslot + i, self.count)
                dr, dc = parity_device(k)
                send_or_keep(k == kslot, self.hs.at[k], self.rsin.at[kslot], self.sem[2], self.sem[3], dr, dc)

            loop(0, self.count, one)

        def gather(self):
            @pl.when(self.reducer)
            def _():
                drain(self.rsin, self.sem[3])
                self.ag[par, kslot] = jnp.sum(self.rsin[...].astype(F32), axis=0).astype(BF)

                def one(i):
                    dr, dc = parity_device(lax.rem(kslot + i, 64))
                    remote(
                        self.ag.at[par, kslot], self.ag.at[par, kslot], self.sem[4], self.sem[5], dr, dc
                    ).start()

                loop(1, 64, one)

        def swap(self):
            @pl.when(self.reducer)
            def _():
                drain(self.ag.at[0, pl.ds(0, self.count - 1)], self.sem[5])
                drain(self.rsin.at[pl.ds(0, 63)], self.sem[4])
                drain(self.hs.at[pl.ds(0, self.count - 1)], self.sem[2])

            @pl.when(jnp.logical_not(self.reducer))
            def _():
                drain(self.ag.at[0, pl.ds(0, self.count)], self.sem[5])
                drain(self.hs, self.sem[2])

            remote(self.ag.at[par], self.ag.at[par], self.sem[6], self.sem[7], mate, c).start()

        def finish(self):
            remote(self.ag.at[par], self.ag.at[par], self.sem[6], self.sem[7], mate, c).wait()

        def put(self, at, value):
            n = value.shape[0] // 16
            half, k = at // self.count, at % self.count
            self.g[half, k : k + n] = value.astype(BF).reshape(n, 16, 128)

        def get(self, at, n):
            half, k = at // self.count, at % self.count
            return self.ag[half, k : k + n].reshape(n * 16, 128).astype(F32)

    early = Total(64, eg, epin, ehs, ersin, eag, 48)
    late = Total(48, lg, lpin, lhs, lrsin, lag, 56)

    zero64 = jnp.zeros((64, 256), BF)
    for h in range(HEADS):
        wq[128 * h : 128 * h + 64] = (wqkv[64 * h : 64 * h + 64].astype(F32) * 0.125).astype(BF)
        wq[128 * h + 64 : 128 * h + 128] = zero64
        wkv[128 * h : 128 * h + 64] = wqkv[256 + 64 * h : 320 + 64 * h]
        wkv[128 * h + 64 : 128 * h + 128] = wqkv[512 + 64 * h : 576 + 64 * h]
    xt = x_ref[...].reshape(256, 256)
    for h in range(HEADS):
        rows = slice(128 * h, 128 * h + 128)
        kv = nt(xt, wkv[rows, :]).astype(BF).reshape(8, 32, 128)
        q = nt(xt, wq[rows, :]).astype(BF).reshape(8, 32, 128)
        for s in range(8):
            kv_send[s * HEADS + h] = kv[s]
            q_send[s * HEADS + h] = q[s]

    to = lax.broadcasted_iota(jnp.int32, (128, 128), 0)
    of = lax.broadcasted_iota(jnp.int32, (128, 128), 1)
    split = (of == (lax.div(to, 64) * 64 + 2 * lax.rem(to, 32) + lax.rem(lax.div(to, 32), 2))).astype(BF)
    merge = (to == (lax.div(of, 64) * 64 + 2 * lax.rem(of, 32) + lax.rem(lax.div(of, 32), 2))).astype(BF)
    eye = (to == of).astype(BF)

    def take_cot(s):
        g = nn(split, cot_ref[s])
        low = g.astype(BF)
        gx[s, 1:3, 1:3] = low.reshape(2, 2, 32, 128)
        gt[s] = nt(eye, low).astype(BF)
        for a in range(2):
            gedge[0, a, pl.ds(s, 1), :] = g[64 * a : 64 * a + 1]
            gedge[1, a, pl.ds(s, 1), :] = g[64 * a + 63 : 64 * a + 64]

    loop(0, 8, take_cot)

    pl.semaphore_wait(barrier, ROWS * COLS - 1)

    def send_kv(i):
        k = lax.rem(kslot + i, 64)
        dr, dc = parity_device(k)
        send_or_keep(
            i == 0, kv_send.at[dc * HEADS + lax.div(dr, 4)], kv_in.at[par, kslot], sems.at[0], sems.at[1], dr, dc
        )

    loop(0, 64, send_kv)
    to_attention(q_send, q_in, sems.at[2], sems.at[3])
    cot_copies = halo_start(gx, gedge, ghalo, 16)

    def take_skip(s):
        pre_ref[s] = nn(split, skip_ref[s])

    loop(0, 8, take_skip)
    halo_finish(gx, ghalo, cot_copies)

    def back_conv(half):
        total = jnp.zeros((512, 128), F32)
        for t, (dr, dc) in enumerate(TAPS):
            window = gx[pl.ds(4 * half, 4), 1 - dr : 3 - dr, 1 - dc : 3 - dc].reshape(512, 128)
            total = total + nn(window, wconv[t])
        dh_ref[pl.ds(4 * half, 4)] = total.reshape(4, 128, 128)

    loop(0, 2, back_conv)

    drain(kv_in.at[par], sems.at[1])
    mate_kv = remote(kv_in.at[par], kv_in.at[par], sems.at[4], sems.at[5], mate, c)
    mate_kv.start()
    drain(q_in, sems.at[3])
    for _ in range(3):
        drain(kv_send.at[pl.ds(0, 21)], sems.at[0])
    drain32(q_send, sems.at[2])
    mate_kv.wait()

    def ones_values(i):
        part = kv_in[lax.div(i, 4), pl.ds(lax.rem(i, 4) * 16, 16)].reshape(512, 128)
        lane = lax.broadcasted_iota(jnp.int32, (512, 128), 1)
        v1[pl.ds(pl.multiple_of(i * 512, 512), 512), :] = jnp.where(lane < 64, jnp.ones_like(part), part)

    loop(0, 8, ones_values)

    def keys(j):
        n = CHUNK // 32
        return kv_in[j * n // 64, (j * n) % 64 : (j * n) % 64 + n].reshape(CHUNK, 128)

    lane = lax.broadcasted_iota(jnp.int32, (BLOCK, 128), 1)

    def forward(b):
        q = q_in[pl.ds(8 * b, 8)].reshape(BLOCK, 128)
        top = None
        for j in range(4096 // CHUNK):
            s = nt(q, keys(j))
            s_ref[:, CHUNK * j : CHUNK * (j + 1)] = s
            for g in range(CHUNK // 128):
                part = s[:, 128 * g : 128 * (g + 1)]
                top = part if top is None else jnp.maximum(top, part)
        m = jnp.max(top, axis=1, keepdims=True)
        acc = jnp.zeros((BLOCK, 128), F32)
        rows = pl.ds(pl.multiple_of(b * BLOCK, BLOCK), BLOCK)
        for j in range(4096 // CHUNK):
            p = jnp.exp(s_ref[:, CHUNK * j : CHUNK * (j + 1)] - m).astype(BF)
            p_ref[rows, CHUNK * j : CHUNK * (j + 1)] = p
            acc = acc + nn(p, v1[CHUNK * j : CHUNK * (j + 1), :])
        inv = 1.0 / jnp.where(lane < 64, 1.0, pltpu.roll(acc, 64, axis=1))
        invl_ref[rows, :] = inv
        o = jnp.where(lane < 64, 0.0, acc * inv).astype(BF)
        o_buf[pl.ds(8 * b, 8)] = o.reshape(8, 32, 128)
        to_cells(o_buf, ocell, sems.at[6], sems.at[7], b)

    loop(0, 1024 // BLOCK, forward)

    levels = fscale.shape[0]
    pick = (noise_col[...] == lax.broadcasted_iota(jnp.int32, (8, levels), 1)).astype(F32)
    exact = lax.Precision.HIGHEST
    scale_rows = 1.0 + jnp.dot(pick, fscale[...], precision=exact, preferred_element_type=F32)
    shift_rows = jnp.dot(pick, fshift[...], precision=exact, preferred_element_type=F32)
    drain(ocell, sems.at[7])
    drain32(o_buf, sems.at[6])
    oc = ocell[...].reshape(8, HEADS, 32, 128)
    branch = xt.astype(F32)
    for h in range(HEADS):
        branch = branch + nt(oc[:, h].reshape(256, 128), woutn[:, 128 * h : 128 * (h + 1)])
    y = branch.astype(BF)
    y_ref[...] = y
    lifted = nt(y, wup[...])
    for s in range(8):
        u = lifted[32 * s : 32 * (s + 1)]
        pre = pre_ref[s] + jnp.concatenate([u, u, u, u], axis=0)
        pre_ref[s] = pre
        act = pre * scale_rows[s : s + 1] + shift_rows[s : s + 1]
        act_ref[s] = act
        low = (act * jax.nn.sigmoid(act)).astype(BF)
        hx[s, 1:3, 1:3] = low.reshape(2, 2, 32, 128)
        wide = low.astype(F32)
        for a in range(2):
            hedge[0, a, s : s + 1, :] = wide[64 * a : 64 * a + 1]
            hedge[1, a, s : s + 1, :] = wide[64 * a + 63 : 64 * a + 64]
    hid_copies = halo_start(hx, hedge, hhalo, 32)

    scale_terms, shift_terms = [], []
    for s in range(8):
        act = act_ref[s]
        sg = jax.nn.sigmoid(act)
        dact = dh_ref[s] * (sg * (1.0 + act * (1.0 - sg)))
        scale_terms.append(jnp.sum(dact * pre_ref[s], axis=0, keepdims=True))
        shift_terms.append(jnp.sum(dact, axis=0, keepdims=True))
        dpre = dact * scale_rows[s : s + 1]
        dh_ref[s] = dpre
        du_ref[32 * s : 32 * (s + 1)] = dpre[0:32] + dpre[32:64] + dpre[64:96] + dpre[96:128]
    du = du_ref[...].astype(BF)
    dy = nn(du, wup[...])
    dy_ref[...] = dy
    low_dy = dy.astype(BF)
    for h in range(HEADS):
        do = nn(low_dy, woutn[:, 128 * h : 128 * (h + 1)]).astype(BF).reshape(8, 32, 128)
        for s in range(8):
            do_send[s * HEADS + h] = do[s]
    to_attention(do_send, do_in, sems.at[8], sems.at[9])

    spread = (noise_row[...] == lax.broadcasted_iota(jnp.int32, (32, 8), 0)).astype(F32)
    early.put(120, jnp.dot(spread, jnp.concatenate(scale_terms, axis=0), precision=exact, preferred_element_type=F32))
    early.put(122, jnp.dot(spread, jnp.concatenate(shift_terms, axis=0), precision=exact, preferred_element_type=F32))
    grad_up = nn(du_ref[...].T.astype(BF), y)
    early.put(72, grad_up[:, 0:128])
    early.put(80, grad_up[:, 128:256])
    dyt = dy.T.astype(BF)
    wide_lane = lax.broadcasted_iota(jnp.int32, (256, 128), 1)
    for g in range(2):
        first = nn(dyt, oc[:, 2 * g].reshape(256, 128))
        second = nn(dyt, oc[:, 2 * g + 1].reshape(256, 128))
        early.put(88 + 16 * g, jnp.where(wide_lane < 64, pltpu.roll(first, 64, axis=1), second))

    halo_finish(hx, hhalo, hid_copies)

    def conv(half):
        total = jnp.zeros((512, 128), F32)
        grads = [gt[4 * half + i] for i in range(4)]
        for t, (dr, dc) in enumerate(TAPS):
            window = hx[pl.ds(4 * half, 4), 1 + dr : 3 + dr, 1 + dc : 3 + dc]
            total = total + nt(window.reshape(512, 128), wconv[t])
            term = None
            for i in range(4):
                one = nn(grads[i], window[i].reshape(128, 128))
                term = one if term is None else term + one
            gacc[t] = jnp.where(half == 0, term, gacc[t] + term)
        low = total.astype(BF)
        for i in range(4):
            dec_ref[4 * half + i] = nn(merge, low[128 * i : 128 * (i + 1)]).astype(BF)
            gskip_ref[4 * half + i] = nn(merge, dh_ref[4 * half + i].astype(BF)).astype(BF)

    gacc[...] = jnp.zeros((9, 128, 128), F32)
    loop(0, 2, conv)
    for t in range(9):
        early.put(8 * t, gacc[t])
    for k in range(124, 128):
        eg[1, k - 64] = jnp.zeros((16, 128), BF)
    early.start()

    dkvt[...] = jnp.zeros((128, 4096), F32)
    drain(do_in, sems.at[9])
    drain32(do_send, sems.at[8])
    early.scatter()

    def backward(b):
        rows = pl.ds(pl.multiple_of(b * BLOCK, BLOCK), BLOCK)
        q = q_in[pl.ds(8 * b, 8)].reshape(BLOCK, 128)
        o = o_buf[pl.ds(8 * b, 8)].reshape(BLOCK, 128).astype(F32)
        do = (do_in[pl.ds(8 * b, 8)].reshape(BLOCK, 128).astype(F32) * invl_ref[rows, :]).astype(BF)
        dof = do.astype(F32)
        delta = -jnp.sum(dof * o, axis=1, keepdims=True)
        high = delta.astype(BF).astype(F32)
        mid = (delta - high).astype(BF).astype(F32)
        rest = delta - high - mid
        ext = jnp.where(lane == 0, high, jnp.where(lane == 1, mid, jnp.where(lane == 2, rest, dof))).astype(BF)
        qt = q.astype(F32).T.astype(BF)
        dot = dof.T.astype(BF)
        dq = jnp.zeros((BLOCK, 128), F32)
        for j in range(4096 // CHUNK):
            cols = slice(CHUNK * j, CHUNK * (j + 1))
            t = nt(ext, v1[cols, :])
            p = p_ref[rows, cols]
            ds = (p.astype(F32) * t).astype(BF)
            dq = dq + nn(ds, keys(j))
            dkvt[:, cols] += nn(qt, ds) + nn(dot, p)
        dq_buf[pl.ds(8 * b, 8)] = dq.astype(BF).reshape(8, 32, 128)
        to_cells(dq_buf, dq_in, sems.at[10], sems.at[11], b)

    loop(0, 2, backward)
    early.gather()
    loop(2, 4, backward)
    early.swap()

    def give(i):
        at = pl.multiple_of((1 - par) * 2048 + i * 512, 512)
        pair_send[pl.ds(16 * i, 16)] = dkvt[:, pl.ds(at, 512)].T.astype(BF).reshape(16, 32, 128)

    loop(0, 4, give)
    swap = remote(pair_send, pair_in, sems.at[12], sems.at[13], mate, c)
    swap.start()
    swap.wait()

    def add(i):
        at = pl.multiple_of(par * 2048 + i * 512, 512)
        mine = dkvt[:, pl.ds(at, 512)].T.reshape(16, 32, 128)
        dkv_send[pl.ds(16 * i, 16)] = (mine + pair_in[pl.ds(16 * i, 16)].astype(F32)).astype(BF)

    loop(0, 4, add)
    zhi = lax.rem(lax.div(r, 2), 2)

    def send_dkv(i):
        k = lax.rem(kslot + i, 64)
        dr, dc = parity_device(k)
        send_or_keep(i == 0, dkv_send.at[k], dkv_in.at[zhi, pair_index], sems.at[14], sems.at[15], dr, dc)

    loop(0, 64, send_dkv)

    early.finish()
    for t in range(9):
        gconv_ref[t] = early.get(8 * t, 8)
    gup_ref[:, 0:128] = early.get(72, 8)
    gup_ref[:, 128:256] = early.get(80, 8)
    gout_ref[:, 0:128] = early.get(88, 16)
    gout_ref[:, 128:256] = early.get(104, 16)
    gscale_ref[...] = early.get(120, 2)[0:levels]
    gshift_ref[...] = early.get(122, 2)[0:levels]

    drain(dq_in, sems.at[11])
    drain32(dq_buf, sems.at[10])
    drain(dkv_in, sems.at[15])
    drain(dkv_send.at[pl.ds(0, 63)], sems.at[14])

    dq_all = dq_in[...].reshape(8, HEADS, 32, 128)
    dkv_all = (dkv_in[0].astype(F32) + dkv_in[1].astype(F32)).astype(BF).reshape(8, HEADS, 32, 128)
    for h in range(HEADS):
        dqt = dq_all[:, h].reshape(256, 128).astype(F32).T.astype(BF)
        dkt = dkv_all[:, h].reshape(256, 128).astype(F32).T.astype(BF)
        gq = nn(dqt, xt)[0:64] * 0.125
        gkv = nn(dkt, xt)
        for g in range(2):
            lanes = slice(128 * g, 128 * (g + 1))
            late.put(48 * g + 4 * h, gq[:, lanes])
            late.put(48 * g + 16 + 4 * h, gkv[0:64, lanes])
            late.put(48 * g + 32 + 4 * h, gkv[64:128, lanes])
    late.start()
    grad = dy_ref[...]
    for h in range(HEADS):
        rows = slice(128 * h, 128 * h + 128)
        grad = grad + nn(dq_all[:, h].reshape(256, 128), wq[rows, :])
        grad = grad + nn(dkv_all[:, h].reshape(256, 128), wkv[rows, :])
    gb_ref[...] = grad.reshape(8, 32, 256)
    late.scatter()
    late.gather()
    late.swap()
    late.finish()
    gqkv_ref[:, 0:128] = late.get(0, 48)
    gqkv_ref[:, 128:256] = late.get(48, 48)


def on_device(
    bottleneck, skip_field, cotangent, noise_level, qkv_weight, out_weight, up_weight, conv_weight,
    film_scale, film_shift,
):
    levels = film_scale.shape[0]
    x = jnp.transpose(bottleneck, (0, 2, 3, 1)).reshape(8, 32, 256)
    skip = jnp.transpose(skip_field, (0, 2, 3, 1)).reshape(8, 128, 128)
    cot = jnp.transpose(cotangent, (0, 2, 3, 1)).reshape(8, 128, 128)
    woutn = jnp.pad(out_weight.reshape(256, HEADS, 64), ((0, 0), (0, 0), (64, 0))).reshape(256, 512)

    def shape(*dims, kind=F32):
        return jax.ShapeDtypeStruct(dims, kind)

    def bf(*dims):
        return pltpu.VMEM(dims, BF)

    def f32(*dims):
        return pltpu.VMEM(dims, F32)

    packet = (32, 32, 128)
    outs = pl.pallas_call(
        kernel,
        out_shape=(
            shape(8, 128, 128, kind=BF), shape(8, 32, 256), shape(8, 128, 128, kind=BF), shape(768, 256),
            shape(256, 256), shape(128, 256), shape(9, 128, 128), shape(levels, 128), shape(levels, 128),
        ),
        in_specs=[VMEM] * 11,
        out_specs=(VMEM,) * 9,
        scratch_shapes=[
            bf(512, 256), bf(512, 256), bf(*packet), bf(*packet), bf(2, 64, 32, 128), bf(*packet),
            bf(4096, 128), f32(BLOCK, 4096), bf(1024, 4096), f32(1024, 128), bf(*packet), bf(*packet),
            bf(8, 4, 4, 32, 128), bf(8, 4, 4, 32, 128), bf(8, 128, 128),
            f32(2, 2, 8, 128), f32(2, 2, 8, 128), f32(2, 3, 2, 8, 128), f32(2, 3, 2, 8, 128),
            f32(8, 128, 128), f32(8, 128, 128), f32(8, 128, 128), bf(256, 256), f32(256, 256), f32(256, 128),
            bf(*packet), bf(*packet), f32(128, 4096), bf(*packet), bf(*packet),
            bf(64, 32, 128), bf(64, 32, 128), bf(64, 32, 128), bf(2, 32, 32, 128), f32(9, 128, 128),
            bf(2, 64, 16, 128), bf(64, 16, 128), bf(64, 16, 128), bf(64, 16, 128), bf(2, 64, 16, 128),
            bf(2, 48, 16, 128), bf(48, 16, 128), bf(48, 16, 128), bf(64, 16, 128), bf(2, 48, 16, 128),
            pltpu.SemaphoreType.DMA((64,)),
        ],
        compiler_params=pltpu.CompilerParams(
            collective_id=0, has_side_effects=True, vmem_limit_bytes=60 * 1024 * 1024
        ),
        name="unet_step",
    )(
        x, skip, cot, noise_level.reshape(8, 1), noise_level.reshape(1, 8), qkv_weight, woutn, up_weight,
        conv_weight, film_scale, film_shift,
    )
    decoded, grad_x, grad_skip = outs[:3]
    return (
        jnp.transpose(decoded.reshape(8, 2, 64, 128), (0, 3, 1, 2)),
        jnp.transpose(grad_x.reshape(8, 1, 32, 256), (0, 3, 1, 2)),
        jnp.transpose(grad_skip.reshape(8, 2, 64, 128), (0, 3, 1, 2)),
    ) + tuple(outs[3:])


def solution(mesh):
    cells = P(None, None, "rows", "cols")
    return jax.shard_map(
        on_device,
        mesh=mesh,
        in_specs=(cells, cells, cells) + (P(),) * 7,
        out_specs=(cells, cells, cells) + (P(),) * 6,
        check_vma=False,
    )
```

time: 494 us -> 121 us (0.24); the launches traced: 486 us -> 121 us
  waiting for transfers between devices: 206 us -> 0 us
  matrix products: 153 us -> 0 us
  Pallas kernels: 0 us -> 108 us
  starting transfers between devices: 69.1 us -> 0 us
  local copies, waits for them, and re-layouts: 31.3 us -> 11.9 us
  between operations: 14.9 us -> 0.69 us
  other arithmetic: 10.7 us -> 0 us
    dot_general x152 -> x0, matrix products: 153 us -> none  [the longest x32 35.3 us: head_scores(): jnp.einsum('sdi,sdj->sij', query_block, keys_block, preferred_element_typ...]
    psum x1 -> x0, waiting for transfers between devices: 139 us -> none  [packed_total(): so_far = lax.psum(flat, axis)]
    pallas_call x0 -> x1, Pallas kernels: none -> 108 us  [on_device(): pl.pallas_call(kernel, out_shape=(shape(8, 128, 128, kind=BF), shape(8, 3...]
    all_to_all x8 -> x0, waiting for transfers between devices: 65.7 us -> none  [the longest x1 34.6 us: on_device(): lax.all_to_all(partial_value, 'rows', split_axis=4, concat_axis=2, tiled=...]
    all_to_all x8 -> x0, starting transfers between devices: 45.1 us -> none  [the longest x1 7.5 us: on_device(): lax.all_to_all(spread, 'rows', split_axis=2, concat_axis=4, tiled=True)]
    ppermute x8 -> x0, starting transfers between devices: 24 us -> none  [the longest x4 14.9 us: with_halo(): lax.ppermute(tail, axis, [(i, (i + 1) % count) for i in range(ends)])]
    slice x12 -> x0, local copies, waits for them, and re-layouts: 9 us -> none  [the longest x8 6.26 us: packed_total(): gathered.append(so_far[at:at + a.size].reshape(a.shape))]
    another operation x2 -> x0, local copies, waits for them, and re-layouts: 5.6 us -> none  [the longest x1 3.47 us: on_device(): jnp.stack([query_buffer, key_buffer, value_buffer], axis=1)]
  transfers between devices with their start and end apart: 17 -> 0, of which waited for: 8 -> 0; matrix products, arithmetic and copies ran while one was open for 19% -> 0% of each run, Pallas kernels for 0% -> 0%
where the time goes in v1:
time: 121 us
  Pallas kernels  108 us (89%)
  local copies, waits for them, and re-layouts  11.9 us (10%)
    pallas_call x1, Pallas kernels, on_device(): pl.pallas_call(kernel, out_shape=(shape(8, 128, 128, kind=BF), shape(8, 3...  108 us
    unnamed x26, local copies, waits for them, and re-layouts  10.4 us

profile of v1, /device:TPU:1, one launch (start us, length us, event | category | flops | bytes accessed | tf_op | source)
XLA Modules:
  0.0 120.9 jit_solution(747585230092851055)
XLA Ops:
  0.6 0.0 copy-start.7
  0.7 0.6 copy-done.7
  1.3 0.7 copy.25.noise_col
  2.0 1.0 copy.23
  3.0 0.8 copy.27.woutn
  3.9 108.3 %unet_step.1 = (bf16[8,128,128]{2,1,0:T(8,128)(2,1)}, f32[8,32,256]{2,1,0:T(8,128)}, bf16[8,128,128]{2,1,0:T(8,128)(2,1)}, f32[768,256]{1,0:T(8,128)}, f32[256,2...) custom-call(bf16[8,32,256]{2,1,0:T(8,128)(2,1)} %bitcast.33, ...), custom_call_target="tpu_custom_call" | custom-call | tf_op jit(solution)/shard_map/unet_step/pallas_call | solution.py:543
  112.2 0.0 copy-start
  112.2 1.7 %copy.37 = bf16[8,128,2,64]{1,3,2,0:T(8,128)(2,1)} copy(bf16[8,128,2,64]{1,3,2,0:T(8,128)(2,1)} %bitcast.32) | data formatting | bytes 524288
  113.9 0.0 copy-start.3
  113.9 1.7 %copy.38 = f32[8,256,1,32]{1,3,2,0:T(8,128)} copy(f32[8,256,1,32]{1,3,2,0:T(8,128)} %bitcast.31) | data formatting | bytes 524288
  115.6 0.0 copy-done.3
  115.6 0.7 copy.39
  116.3 0.0 copy-done
  116.3 0.0 copy-start.2
  116.3 0.0 copy-start.4
  116.3 0.9 copy.40
  117.2 0.2 copy-done.2
  117.4 0.0 copy-start.1
  117.4 0.7 copy.41
  118.1 0.0 copy-done.4
  118.1 0.7 copy.42
  118.8 0.0 copy-done.1
  118.8 0.0 copy-start.6
  118.8 0.8 copy.43
  119.6 0.0 copy-done.6
  119.6 0.0 copy-start.5
  119.6 0.6 copy.44
  120.2 0.1 copy-done.5
  120.3 0.6 copy.45
  (1 shorter events, 0.0 us)
Async XLA Ops:
  0.6 0.7 copy-start.7
  112.2 4.2 %copy-start = (f32[768,256]{1,0:T(8,128)S(1)}, f32[768,256]{1,0:T(8,128)}, u32[]{:S(2)}) copy-start(f32[768,256]{1,0:T(8,128)} %get-tuple-element.57) | copy-start | bytes 2359300
  113.9 1.7 %copy-start.3 = (bf16[8,128,128]{2,1,0:T(8,128)(2,1)S(1)}, bf16[8,128,128]{2,1,0:T(8,128)(2,1)}, u32[]{:S(2)}) copy-start(bf16[8,128,128]{2,1,0:T(8,128)(2,1)} %get-tuple-element.20) | copy-start | bytes 786436
  116.3 1.1 copy-start.2
  116.3 1.8 %copy-start.4 = (f32[128,256]{1,0:T(8,128)S(1)}, f32[128,256]{1,0:T(8,128)}, u32[]{:S(2)}) copy-start(f32[128,256]{1,0:T(8,128)} %get-tuple-element.59) | copy-start | bytes 393220
  117.4 1.4 %copy-start.1 = (f32[9,128,128]{2,1,0:T(8,128)S(1)}, f32[9,128,128]{2,1,0:T(8,128)}, u32[]{:S(2)}) copy-start(f32[9,128,128]{2,1,0:T(8,128)} %get-tuple-element.60) | copy-start | bytes 1769476
  118.8 0.8 copy-start.6
  119.6 0.7 copy-start.5

commit v2 on v1

v2 whole, which is shorter than its diff:
```python
import functools

import jax
import jax.numpy as jnp
from jax import lax
from jax.experimental import pallas as pl
from jax.experimental.pallas import tpu as pltpu
from jax.sharding import PartitionSpec as P

MESH = pl.DeviceIdType.MESH
BF = jnp.bfloat16
F32 = jnp.float32
ROWS, COLS = 16, 8
HEADS = 4
BLOCK = 256
CHUNK = 1024
TAPS = [(-1, -1), (-1, 0), (-1, 1), (0, -1), (0, 0), (0, 1), (1, -1), (1, 0), (1, 1)]
VMEM = pl.BlockSpec(memory_space=pltpu.VMEM)


def nn(a, b):
    return lax.dot_general(a, b, (((1,), (0,)), ((), ())), preferred_element_type=F32)


def nt(a, b):
    return lax.dot_general(a, b, (((1,), (1,)), ((), ())), preferred_element_type=F32)


def remote(src, dst, send, recv, row, col):
    return pltpu.make_async_remote_copy(
        src_ref=src, dst_ref=dst, send_sem=send, recv_sem=recv, device_id=(row, col), device_id_type=MESH
    )


def send_or_keep(here, src, dst, send, recv, row, col):
    @pl.when(here)
    def _():
        pltpu.make_async_copy(src, dst, recv).start()

    @pl.when(jnp.logical_not(here))
    def _():
        remote(src, dst, send, recv, row, col).start()


def drain(ref, sem):
    pltpu.make_async_copy(ref, ref, sem).wait()


def loop(lo, hi, body):
    def step(i, carry):
        body(i)
        return carry

    lax.fori_loop(lo, hi, step, 0)


def kernel(
    noise, x_ref, skip_ref, cot_ref, wqkv, wout, wup, wconv, fscale, fshift,
    dec_ref, gb_ref, gskip_ref, eag, lag,
    woutn, wq, wkv, kv_send, q_send, kv_in, q_fold, q_in, v1, xall, s_ref, p_ref, invl_ref, o_buf, o_send, o_fold,
    ocell, gx, hx, gt, gedge, hedge, ghalo, hhalo, pre_ref, act_ref, dh_ref, dy_ref, du_ref,
    do_send, do_fold, ext_ref, qt_ref, dot_ref, dkvt, dq_acc, dq_send, dq_fold, dq_in, pair_send, pair_in, dkv_send,
    dkv_in, gacc, gkv, eg, epin, ehs, ersin, lg, lrs, sems,
):
    r, c = lax.axis_index("rows"), lax.axis_index("cols")
    par = lax.rem(r, 2)
    mate = r + 1 - 2 * par
    pair = lax.div(r, 2)
    kslot = pair * COLS + c
    head, quarter = lax.div(r, 4), lax.rem(r, 4)
    qslot = quarter * COLS + c
    own = head == quarter
    spot = c * HEADS + head
    cols = [lax.rem(c + j, COLS) for j in range(COLS)]

    barrier = pltpu.get_barrier_semaphore()

    def signal(row, dc):
        pl.semaphore_signal(barrier, inc=1, device_id=(row, dc), device_id_type=MESH)

    for j in range(1, COLS):
        signal(r, cols[j])

    def signal_row(i):
        row = lax.rem(r + i, ROWS)
        for j in range(COLS):
            signal(row, cols[j])

    loop(1, ROWS, signal_row)

    def to_attention(src, dst, send, recv):
        def row(i):
            h = lax.rem(head + i, HEADS)
            dr = HEADS * h + head
            send_or_keep((i == 0) & own, src.at[c * HEADS + h], dst.at[qslot], send, recv, dr, c)
            for j in range(1, COLS):
                remote(src.at[cols[j] * HEADS + h], dst.at[qslot], send, recv, dr, cols[j]).start()

        loop(0, HEADS, row)

    def to_cells(src, dst, send, recv, row):
        dr = 4 * quarter + row
        send_or_keep(dr == r, src.at[row * COLS + c], dst.at[spot], send, recv, dr, c)
        for j in range(1, COLS):
            remote(src.at[row * COLS + cols[j]], dst.at[spot], send, recv, dr, cols[j]).start()

    def drain32(ref, sem):
        @pl.when(own)
        def _():
            drain(ref.at[pl.ds(0, 31)], sem)

        @pl.when(jnp.logical_not(own))
        def _():
            drain(ref, sem)

    def to_parity(lo, hi, source, target, send, recv, first=0, last=COLS):
        def row(i):
            at = lax.rem(pair + i, 8)
            dr = 2 * at + par
            for j in range(first, last):
                src = source(at, cols[j])
                if j == 0:
                    send_or_keep(i == 0, src, target, send, recv, dr, c)
                else:
                    remote(src, target, send, recv, dr, cols[j]).start()

        loop(lo, hi, row)

    def halo_start(ext, edge, halo, base):
        up, down = lax.rem(r + ROWS - 1, ROWS), lax.rem(r + 1, ROWS)
        left, right = cols[COLS - 1], cols[1]
        copies = [
            remote(ext.at[:, 1, pl.ds(1, 2)], ext.at[:, 3, pl.ds(1, 2)], sems.at[base], sems.at[base + 1], up, c),
            remote(ext.at[:, 2, pl.ds(1, 2)], ext.at[:, 0, pl.ds(1, 2)], sems.at[base + 2], sems.at[base + 3], down, c),
        ]
        at = base + 4
        for row, slot in ((up, 2), (r, 1), (down, 0)):
            copies.append(remote(edge.at[0], halo.at[1, slot], sems.at[at], sems.at[at + 1], row, left))
            copies.append(remote(edge.at[1], halo.at[0, slot], sems.at[at + 2], sems.at[at + 3], row, right))
            at += 4
        for copy in copies:
            copy.start()
        return copies

    def halo_finish(ext, halo, copies):
        for copy in copies:
            copy.wait()

        @pl.when(r == 0)
        def _():
            ext[:, 0, 1:3] = jnp.zeros((8, 2, 32, 128), BF)
            halo[:, 0] = jnp.zeros((2, 2, 8, 128), F32)

        @pl.when(r == ROWS - 1)
        def _():
            ext[:, 3, 1:3] = jnp.zeros((8, 2, 32, 128), BF)
            halo[:, 2] = jnp.zeros((2, 2, 8, 128), F32)

        @pl.when(c == 0)
        def _():
            halo[0] = jnp.zeros((3, 2, 8, 128), F32)

        @pl.when(c == COLS - 1)
        def _():
            halo[1] = jnp.zeros((3, 2, 8, 128), F32)

        place = lax.broadcasted_iota(jnp.int32, (32, 128), 0)

        def one(s):
            for row, (slot, a) in enumerate(((0, 1), (1, 0), (1, 1), (2, 0))):
                odd = ext[s, row, 2].astype(F32)
                even = ext[s, row, 1].astype(F32)
                before = halo[0, slot, a, pl.ds(s, 1), :]
                after = halo[1, slot, a, pl.ds(s, 1), :]
                ext[s, row, 0] = jnp.where(place == 0, before, pltpu.roll(odd, 1, axis=0)).astype(BF)
                ext[s, row, 3] = jnp.where(place == 31, after, pltpu.roll(even, 31, axis=0)).astype(BF)

        loop(0, 8, one)

    esem = [sems.at[48 + i] for i in range(8)]

    def early_put(at, value):
        n = value.shape[0] // 16
        eg[at // 64, at % 64 : at % 64 + n] = value.astype(BF).reshape(n, 16, 128)

    def early_halves():
        return remote(eg.at[1 - par], epin, esem[0], esem[1], mate, c)

    def early_scatter():
        early_halves().wait()
        ehs[...] = (eg[par].astype(F32) + epin[...].astype(F32)).astype(BF)
        to_parity(0, 8, lambda at, dc: ehs.at[at * COLS + dc], ersin.at[kslot], esem[2], esem[3])

    def early_gather():
        drain(ersin, esem[3])
        eag[par, kslot] = jnp.sum(ersin[...].astype(F32), axis=0).astype(BF)
        mine = eag.at[par, kslot]
        for j in range(1, COLS):
            remote(mine, mine, esem[4], esem[5], r, cols[j]).start()
        def row(i):
            dr = 2 * lax.rem(pair + i, 8) + par
            for j in range(COLS):
                remote(mine, mine, esem[4], esem[5], dr, cols[j]).start()

        loop(1, 8, row)

    def early_swap():
        return remote(eag.at[par], eag.at[par], esem[6], esem[7], mate, c)

    def early_drain():
        drain(eag.at[0, pl.ds(0, 63)], esem[5])
        drain(ersin.at[pl.ds(0, 63)], esem[4])
        drain(ehs.at[pl.ds(0, 63)], esem[2])

    low_lane = lax.broadcasted_iota(jnp.int32, (BLOCK, 128), 1) < 64

    def half_turn(value):
        return pltpu.roll(value, 64, axis=1)

    def fold_low(value):
        cut = value.reshape(8, 32, 128)
        first, second = cut[:, 0:16].reshape(128, 128), cut[:, 16:32].reshape(128, 128)
        return jnp.where(low_lane[0:128], first, half_turn(second)).reshape(8, 16, 128)

    def fold_high(value):
        cut = value.reshape(8, 32, 128)
        first, second = cut[:, 0:16].reshape(128, 128), cut[:, 16:32].reshape(128, 128)
        return jnp.where(low_lane[0:128], half_turn(first), second).reshape(8, 16, 128)

    def unfold(src, dst, high, clear):
        def some(i):
            at = pl.ds(8 * i, 8)
            flat = src[at].reshape(128, 128).astype(F32)
            turned = half_turn(flat)
            first, second = (turned, flat) if high else (flat, turned)
            if clear:
                keep = jnp.logical_not(low_lane[0:128]) if high else low_lane[0:128]
                first, second = jnp.where(keep, first, 0.0), jnp.where(keep, second, 0.0)
            dst[at, 0:16] = first.astype(BF).reshape(8, 16, 128)
            dst[at, 16:32] = second.astype(BF).reshape(8, 16, 128)

        loop(0, 4, some)

    zero64 = jnp.zeros((64, 256), BF)
    for h in range(HEADS):
        wq[128 * h : 128 * h + 64] = (wqkv[64 * h : 64 * h + 64].astype(F32) * 0.125).astype(BF)
        wq[128 * h + 64 : 128 * h + 128] = zero64
        wkv[128 * h : 128 * h + 64] = wqkv[256 + 64 * h : 320 + 64 * h]
        wkv[128 * h + 64 : 128 * h + 128] = wqkv[512 + 64 * h : 576 + 64 * h]
    xt = x_ref[...].reshape(256, 256)
    for h in range(HEADS):
        rows = slice(128 * h, 128 * h + 128)
        kv = nt(xt, wkv[rows, :]).astype(BF).reshape(8, 32, 128)
        q = fold_low(nt(xt, wq[rows, :])).astype(BF)
        for s in range(8):
            kv_send[s * HEADS + h] = kv[s]
            q_send[s * HEADS + h] = q[s]

    to = lax.broadcasted_iota(jnp.int32, (128, 128), 0)
    of = lax.broadcasted_iota(jnp.int32, (128, 128), 1)
    split = (of == (lax.div(to, 64) * 64 + 2 * lax.rem(to, 32) + lax.rem(lax.div(to, 32), 2))).astype(BF)
    merge = (to == (lax.div(of, 64) * 64 + 2 * lax.rem(of, 32) + lax.rem(lax.div(of, 32), 2))).astype(BF)
    eye = (to == of).astype(BF)

    def take_cot(s):
        g = nn(split, cot_ref[s])
        low = g.astype(BF)
        gx[s, 1:3, 1:3] = low.reshape(2, 2, 32, 128)
        gt[s] = nt(eye, low).astype(BF)
        for a in range(2):
            gedge[0, a, pl.ds(s, 1), :] = g[64 * a : 64 * a + 1]
            gedge[1, a, pl.ds(s, 1), :] = g[64 * a + 63 : 64 * a + 64]

    pl.semaphore_wait(barrier, ROWS * COLS - 1)
    to_parity(
        0, 8, lambda at, dc: kv_send.at[dc * HEADS + lax.div(at, 2)], kv_in.at[par, kslot], sems.at[0], sems.at[1]
    )
    to_attention(q_send, q_fold, sems.at[2], sems.at[3])
    loop(0, 8, take_cot)
    cot_copies = halo_start(gx, gedge, ghalo, 16)

    def take_skip(s):
        pre_ref[s] = nn(split, skip_ref[s])

    loop(0, 8, take_skip)
    for g in range(2):
        block = wout[:, 128 * g : 128 * (g + 1)].astype(F32)
        woutn[:, 256 * g : 256 * g + 128] = jnp.where(low_lane, 0.0, half_turn(block)).astype(BF)
        woutn[:, 256 * g + 128 : 256 * g + 256] = jnp.where(low_lane, 0.0, block).astype(BF)
    halo_finish(gx, ghalo, cot_copies)

    def back_conv(half):
        total = jnp.zeros((512, 128), F32)
        for t, (dr, dc) in enumerate(TAPS):
            window = gx[pl.ds(4 * half, 4), 1 - dr : 3 - dr, 1 - dc : 3 - dc].reshape(512, 128)
            total = total + nn(window, wconv[t])
        dh_ref[pl.ds(4 * half, 4)] = total.reshape(4, 128, 128)

    loop(0, 2, back_conv)

    drain(kv_in.at[par], sems.at[1])
    mate_kv = remote(kv_in.at[par], kv_in.at[par], sems.at[4], sems.at[5], mate, c)
    mate_kv.start()
    drain(q_fold, sems.at[3])
    unfold(q_fold, q_in, False, True)
    for _ in range(3):
        drain(kv_send.at[pl.ds(0, 21)], sems.at[0])
    drain32(q_send, sems.at[2])

    def ones_values(half):
        def some(i):
            part = kv_in[half, pl.ds(i * 16, 16)].reshape(512, 128)
            lane = lax.broadcasted_iota(jnp.int32, (512, 128), 1)
            at = pl.multiple_of(half * 2048 + i * 512, 512)
            v1[pl.ds(at, 512), :] = jnp.where(lane < 64, jnp.ones_like(part), part)

        loop(0, 4, some)

    ones_values(par)
    mate_kv.wait()
    ones_values(1 - par)
    to_parity(0, 8, lambda at, dc: x_ref.at[dc], xall.at[par, kslot], sems.at[60], sems.at[61], 0, 4)

    def keys(j):
        n = CHUNK // 32
        return kv_in[j * n // 64, (j * n) % 64 : (j * n) % 64 + n].reshape(CHUNK, 128)

    def forward(b):
        q = q_in[pl.ds(8 * b, 8)].reshape(BLOCK, 128)
        top = None
        for j in range(4096 // CHUNK):
            s = nt(q, keys(j))
            s_ref[:, CHUNK * j : CHUNK * (j + 1)] = s
            for g in range(CHUNK // 128):
                part = s[:, 128 * g : 128 * (g + 1)]
                top = part if top is None else jnp.maximum(top, part)
        m = jnp.max(top, axis=1, keepdims=True)
        acc = jnp.zeros((BLOCK, 128), F32)
        rows = pl.ds(pl.multiple_of(b * BLOCK, BLOCK), BLOCK)
        for j in range(4096 // CHUNK):
            p = jnp.exp(s_ref[:, CHUNK * j : CHUNK * (j + 1)] - m).astype(BF)
            p_ref[rows, CHUNK * j : CHUNK * (j + 1)] = p
            acc = acc + nn(p, v1[CHUNK * j : CHUNK * (j + 1), :])
        inv = 1.0 / jnp.where(low_lane, 1.0, half_turn(acc))
        invl_ref[rows, :] = inv
        o = jnp.where(low_lane, 0.0, acc * inv)
        o_buf[rows, :] = o.astype(BF)
        o_send[pl.ds(8 * b, 8)] = fold_high(o).astype(BF)
        to_cells(o_send, o_fold, sems.at[6], sems.at[7], b)

    loop(0, 1024 // BLOCK, forward)
    to_parity(0, 8, lambda at, dc: x_ref.at[dc], xall.at[par, kslot], sems.at[60], sems.at[61], 4, 8)

    levels = fscale.shape[0]
    level = lax.broadcasted_iota(jnp.int32, (levels, 128), 0)
    scales, shifts = [], []
    for s in range(8):
        here = level == noise[s]
        scales.append(1.0 + jnp.sum(jnp.where(here, fscale[...], 0.0), axis=0, keepdims=True))
        shifts.append(jnp.sum(jnp.where(here, fshift[...], 0.0), axis=0, keepdims=True))
    drain(o_fold, sems.at[7])
    drain32(o_send, sems.at[6])
    unfold(o_fold, ocell, True, False)
    oc = ocell[...].reshape(8, HEADS, 32, 128)
    branch = xt.astype(F32)
    for h in range(HEADS):
        branch = branch + nt(oc[:, h].reshape(256, 128), woutn[:, 128 * h : 128 * (h + 1)])
    y = branch.astype(BF)
    lifted = nt(y, wup[...])
    for s in range(8):
        u = lifted[32 * s : 32 * (s + 1)]
        pre = pre_ref[s] + jnp.concatenate([u, u, u, u], axis=0)
        pre_ref[s] = pre
        act = pre * scales[s] + shifts[s]
        act_ref[s] = act
        low = (act * jax.nn.sigmoid(act)).astype(BF)
        hx[s, 1:3, 1:3] = low.reshape(2, 2, 32, 128)
        wide = low.astype(F32)
        for a in range(2):
            hedge[0, a, s : s + 1, :] = wide[64 * a : 64 * a + 1]
            hedge[1, a, s : s + 1, :] = wide[64 * a + 63 : 64 * a + 64]
    hid_copies = halo_start(hx, hedge, hhalo, 32)

    spread = lax.broadcasted_iota(jnp.int32, (32, 128), 0)
    scale_sum, shift_sum = jnp.zeros((32, 128), F32), jnp.zeros((32, 128), F32)
    for s in range(8):
        act = act_ref[s]
        sg = jax.nn.sigmoid(act)
        dact = dh_ref[s] * (sg * (1.0 + act * (1.0 - sg)))
        here = spread == noise[s]
        scale_sum += jnp.where(here, jnp.sum(dact * pre_ref[s], axis=0, keepdims=True), 0.0)
        shift_sum += jnp.where(here, jnp.sum(dact, axis=0, keepdims=True), 0.0)
        dpre = dact * scales[s]
        dh_ref[s] = dpre
        du_ref[32 * s : 32 * (s + 1)] = dpre[0:32] + dpre[32:64] + dpre[64:96] + dpre[96:128]
    du = du_ref[...].astype(BF)
    dy = nn(du, wup[...])
    dy_ref[...] = dy
    low_dy = dy.astype(BF)
    for h in range(HEADS):
        do = fold_high(nn(low_dy, woutn[:, 128 * h : 128 * (h + 1)])).astype(BF)
        for s in range(8):
            do_send[s * HEADS + h] = do[s]
    to_attention(do_send, do_fold, sems.at[8], sems.at[9])

    early_put(120, scale_sum)
    early_put(122, shift_sum)
    grad_up = nn(du_ref[...].T.astype(BF), y)
    early_put(72, grad_up[:, 0:128])
    early_put(80, grad_up[:, 128:256])
    dyt = dy.T.astype(BF)
    for g in range(2):
        first = nn(dyt, oc[:, 2 * g].reshape(256, 128))
        second = nn(dyt, oc[:, 2 * g + 1].reshape(256, 128))
        early_put(88 + 16 * g, jnp.where(low_lane, half_turn(first), second))

    halo_finish(hx, hhalo, hid_copies)

    def conv(half):
        total = jnp.zeros((512, 128), F32)
        grads = [gt[4 * half + i] for i in range(4)]
        for t, (dr, dc) in enumerate(TAPS):
            window = hx[pl.ds(4 * half, 4), 1 + dr : 3 + dr, 1 + dc : 3 + dc]
            total = total + nt(window.reshape(512, 128), wconv[t])
            term = None
            for i in range(4):
                one = nn(grads[i], window[i].reshape(128, 128))
                term = one if term is None else term + one
            gacc[t] = gacc[t] + term
        low = total.astype(BF)
        for i in range(4):
            dec_ref[4 * half + i] = nn(merge, low[128 * i : 128 * (i + 1)]).astype(BF)
            gskip_ref[4 * half + i] = nn(merge, dh_ref[4 * half + i].astype(BF)).astype(BF)

    gacc[...] = jnp.zeros((9, 128, 128), F32)
    loop(0, 2, conv)
    for t in range(9):
        early_put(8 * t, gacc[t])
    for k in range(124, 128):
        eg[1, k - 64] = jnp.zeros((16, 128), BF)
    early_halves().start()

    drain(xall.at[par], sems.at[61])
    mate_x = remote(xall.at[par], xall.at[par], sems.at[62], sems.at[63], mate, c)
    mate_x.start()
    drain(xall.at[par, pl.ds(0, 63)], sems.at[60])

    drain(do_fold, sems.at[9])
    drain32(do_send, sems.at[8])
    unfold(do_fold, ocell, True, True)
    lane = lax.broadcasted_iota(jnp.int32, (BLOCK, 128), 1)

    def prepare(b):
        rows = pl.ds(pl.multiple_of(b * BLOCK, BLOCK), BLOCK)
        q = q_in[pl.ds(8 * b, 8)].reshape(BLOCK, 128)
        do = (ocell[pl.ds(8 * b, 8)].reshape(BLOCK, 128).astype(F32) * invl_ref[rows, :]).astype(BF)
        dof = do.astype(F32)
        delta = -jnp.sum(dof * o_buf[rows, :].astype(F32), axis=1, keepdims=True)
        high = delta.astype(BF).astype(F32)
        mid = (delta - high).astype(BF).astype(F32)
        rest = delta - high - mid
        ext = jnp.where(lane == 0, high, jnp.where(lane == 1, mid, jnp.where(lane == 2, rest, dof)))
        ext_ref[rows, :] = ext.astype(BF)
        qt_ref[b] = q.astype(F32).T.astype(BF)
        dot_ref[b] = dof.T.astype(BF)
        dq_acc[rows, :] = jnp.zeros((BLOCK, 128), F32)

    loop(0, 4, prepare)
    gkv[...] = jnp.zeros((256, 256), F32)
    early_scatter()
    mate_x.wait()

    def backward(half, j):
        at = pl.multiple_of(half * 2048 + j * CHUNK, CHUNK)
        kc = kv_in[half, pl.ds(32 * j, 32)].reshape(CHUNK, 128)
        vc = v1[pl.ds(at, CHUNK), :]
        for b in range(4):
            rows = slice(BLOCK * b, BLOCK * (b + 1))
            p = p_ref[rows, pl.ds(at, CHUNK)]
            ds = (p.astype(F32) * nt(ext_ref[rows, :], vc)).astype(BF)
            dq_acc[rows, :] += nn(ds, kc)
            part = nn(qt_ref[b], ds) + nn(dot_ref[b], p)
            dkvt[...] = part if b == 0 else dkvt[...] + part
        xc = xall[half, pl.ds(32 * j, 32)].reshape(CHUNK, 256)
        gkv[0:128] += nn(dkvt[...].astype(BF), xc)
        return dkvt[...].T.reshape(32, 32, 128)

    def pair_copy(j):
        at = pl.ds(32 * j, 32)
        return remote(pair_send.at[at], pair_in.at[at], sems.at[10 + j], sems.at[12 + j], mate, c)

    def mate_chunk(j):
        pair_send[pl.ds(32 * j, 32)] = backward(1 - par, j).astype(BF)
        pair_copy(j).start()

    loop(0, 2, mate_chunk)
    early_gather()
    zhi = lax.rem(pair, 2)

    def own_chunk(j):
        part = backward(par, j)
        pair_copy(j).wait()
        at = pl.ds(32 * j, 32)
        dkv_send[at] = (part + pair_in[at].astype(F32)).astype(BF)
        target = dkv_in.at[zhi, spot]

        def row(i):
            rp = 4 * j + lax.rem(pair + i, 4)
            dr = 2 * rp + par
            send_or_keep(rp == pair, dkv_send.at[rp * COLS + c], target, sems.at[14], sems.at[15], dr, c)
            for k in range(1, COLS):
                remote(dkv_send.at[rp * COLS + cols[k]], target, sems.at[14], sems.at[15], dr, cols[k]).start()

        loop(0, 4, row)

    loop(0, 2, own_chunk)

    def give_dq(b):
        rows = pl.ds(pl.multiple_of(b * BLOCK, BLOCK), BLOCK)
        dq = dq_acc[rows, :]
        dq_send[pl.ds(8 * b, 8)] = fold_low(dq).astype(BF)
        to_cells(dq_send, dq_fold, sems.at[56], sems.at[57], b)
        xq = xall[lax.rem(b, 2), pl.ds(COLS * (2 * quarter + lax.div(b, 2)), COLS)].reshape(BLOCK, 256)
        gkv[128:256] += nn(dq.T.astype(BF), xq)

    loop(0, 4, give_dq)

    for g in range(2):
        lanes = slice(128 * g, 128 * (g + 1))
        for part, (lo, factor) in enumerate(((128, 0.125), (0, 1.0), (64, 1.0))):
            piece = (gkv[lo : lo + 64, lanes] * factor).astype(BF)
            lg[12 * g + 4 * part : 12 * g + 4 * part + 4] = piece.reshape(4, 16, 128)

    def send_lg(i):
        dr = HEADS * head + i
        send_or_keep(quarter == i, lg.at[i * COLS + c], lrs.at[qslot], sems.at[58], sems.at[59], dr, c)
        for j in range(1, COLS):
            remote(lg.at[i * COLS + cols[j]], lrs.at[qslot], sems.at[58], sems.at[59], dr, cols[j]).start()

    loop(0, 3, send_lg)
    early_drain()
    last_swap = early_swap()
    last_swap.start()

    @pl.when(quarter < 3)
    def _():
        drain(lrs, sems.at[59])
        mine = lag.at[head * 24 + qslot]
        lag[head * 24 + qslot] = jnp.sum(lrs[...].astype(F32), axis=0).astype(BF)
        for j in range(1, COLS):
            remote(mine, mine, sems.at[64], sems.at[65], r, cols[j]).start()

        def row(i):
            dr = lax.rem(r + i, ROWS)
            for j in range(COLS):
                remote(mine, mine, sems.at[64], sems.at[65], dr, cols[j]).start()

        loop(1, ROWS, row)

    drain(dq_fold, sems.at[57])
    drain32(dq_send, sems.at[56])
    unfold(dq_fold, dq_in, False, False)
    drain(dkv_in, sems.at[15])
    drain(dkv_send.at[pl.ds(0, 63)], sems.at[14])
    dq_all = dq_in[...].reshape(8, HEADS, 32, 128)
    dkv_all = (dkv_in[0].astype(F32) + dkv_in[1].astype(F32)).astype(BF).reshape(8, HEADS, 32, 128)
    grad = dy_ref[...]
    for h in range(HEADS):
        rows = slice(128 * h, 128 * h + 128)
        grad = grad + nn(dq_all[:, h].reshape(256, 128), wq[rows, :])
        grad = grad + nn(dkv_all[:, h].reshape(256, 128), wkv[rows, :])
    gb_ref[...] = grad.reshape(8, 32, 256)
    last_swap.wait()

    @pl.when(quarter < 3)
    def _():
        drain(lag.at[pl.ds(0, 95)], sems.at[65])
        drain(lg.at[pl.ds(0, 23)], sems.at[58])
        for _ in range(3):
            drain(lrs, sems.at[64])
        drain(lrs.at[pl.ds(0, 31)], sems.at[64])

    @pl.when(quarter == 3)
    def _():
        drain(lag, sems.at[65])
        drain(lg, sems.at[58])


def unpack(dec, gb, gskip, eag, lag, dec_ref, gb_ref, gskip_ref, gqkv_ref, gout_ref, gup_ref, gconv_ref, gscale_ref, gshift_ref):
    dec_ref[...] = dec[...]
    gb_ref[...] = gb[...]
    gskip_ref[...] = gskip[...]

    def early(at, n):
        return eag[at // 64, at % 64 : at % 64 + n].reshape(n * 16, 128).astype(F32)

    for t in range(9):
        gconv_ref[t] = early(8 * t, 8)
    levels = gscale_ref.shape[0]
    gscale_ref[...] = early(120, 2)[0:levels]
    gshift_ref[...] = early(122, 2)[0:levels]
    for g in range(2):
        lanes = slice(128 * g, 128 * (g + 1))
        gup_ref[:, lanes] = early(72 + 8 * g, 8)
        gout_ref[:, lanes] = early(88 + 16 * g, 16)
        for part in range(3):
            for h in range(HEADS):
                at = 24 * h + 12 * g + 4 * part
                rows = slice(256 * part + 64 * h, 256 * part + 64 * h + 64)
                gqkv_ref[rows, lanes] = lag[at : at + 4].reshape(64, 128).astype(F32)


def on_device(
    bottleneck, skip_field, cotangent, noise_level, qkv_weight, out_weight, up_weight, conv_weight,
    film_scale, film_shift,
):
    levels = film_scale.shape[0]
    x = jnp.transpose(bottleneck, (0, 2, 3, 1)).reshape(8, 32, 256)
    skip = jnp.transpose(skip_field, (0, 2, 3, 1)).reshape(8, 128, 128)
    cot = jnp.transpose(cotangent, (0, 2, 3, 1)).reshape(8, 128, 128)

    def shape(*dims, kind=F32):
        return jax.ShapeDtypeStruct(dims, kind)

    def bf(*dims):
        return pltpu.VMEM(dims, BF)

    def f32(*dims):
        return pltpu.VMEM(dims, F32)

    packet, folded = (32, 32, 128), (32, 16, 128)
    cells, packed = shape(8, 128, 128, kind=BF), shape(8, 32, 256)
    parts = pl.pallas_call(
        kernel,
        out_shape=(cells, packed, cells, shape(2, 64, 16, 128, kind=BF), shape(96, 16, 128, kind=BF)),
        in_specs=[pl.BlockSpec(memory_space=pltpu.SMEM)] + [VMEM] * 9,
        out_specs=(VMEM,) * 5,
        scratch_shapes=[
            bf(256, 512), bf(512, 256), bf(512, 256), bf(*packet), bf(*folded), bf(2, 64, 32, 128), bf(*folded),
            bf(*packet), bf(4096, 128), bf(2, 64, 32, 256), f32(BLOCK, 4096), bf(1024, 4096), f32(1024, 128),
            bf(1024, 128), bf(*folded), bf(*folded),
            bf(*packet), bf(8, 4, 4, 32, 128), bf(8, 4, 4, 32, 128), bf(8, 128, 128),
            f32(2, 2, 8, 128), f32(2, 2, 8, 128), f32(2, 3, 2, 8, 128), f32(2, 3, 2, 8, 128),
            f32(8, 128, 128), f32(8, 128, 128), f32(8, 128, 128), f32(256, 256), f32(256, 128),
            bf(*folded), bf(*folded), bf(1024, 128), bf(4, 128, 256), bf(4, 128, 256), f32(128, CHUNK),
            f32(1024, 128), bf(*folded), bf(*folded), bf(*packet),
            bf(64, 32, 128), bf(64, 32, 128), bf(64, 32, 128), bf(2, 32, 32, 128), f32(9, 128, 128), f32(256, 256),
            bf(2, 64, 16, 128), bf(64, 16, 128), bf(64, 16, 128), bf(64, 16, 128),
            bf(24, 16, 128), bf(32, 16, 128),
            pltpu.SemaphoreType.DMA((72,)),
        ],
        compiler_params=pltpu.CompilerParams(
            collective_id=0, has_side_effects=True, vmem_limit_bytes=44 * 1024 * 1024
        ),
        name="unet_step",
    )(noise_level, x, skip, cot, qkv_weight, out_weight, up_weight, conv_weight, film_scale, film_shift)
    outs = pl.pallas_call(
        unpack,
        out_shape=(
            cells, packed, cells, shape(768, 256), shape(256, 256), shape(128, 256), shape(9, 128, 128),
            shape(levels, 128), shape(levels, 128),
        ),
        in_specs=[VMEM] * 5,
        out_specs=(VMEM,) * 9,
        compiler_params=pltpu.CompilerParams(vmem_limit_bytes=16 * 1024 * 1024),
        name="unpack",
    )(*parts)
    decoded, grad_x, grad_skip = outs[:3]
    return (
        jnp.transpose(decoded.reshape(8, 2, 64, 128), (0, 3, 1, 2)),
        jnp.transpose(grad_x.reshape(8, 1, 32, 256), (0, 3, 1, 2)),
        jnp.transpose(grad_skip.reshape(8, 2, 64, 128), (0, 3, 1, 2)),
    ) + tuple(outs[3:])


def solution(mesh):
    cells = P(None, None, "rows", "cols")
    return jax.shard_map(
        on_device,
        mesh=mesh,
        in_specs=(cells, cells, cells) + (P(),) * 7,
        out_specs=(cells, cells, cells) + (P(),) * 6,
        check_vma=False,
    )
```

time: 121 us -> 104 us (0.86)
  Pallas kernels: 108 us -> 94.7 us
  local copies, waits for them, and re-layouts: 11.9 us -> 8.56 us
    pallas_call x1 -> x2, Pallas kernels: 108 us -> 94.7 us  [the longest x1 93.1 us: on_device(): pl.pallas_call(kernel, out_shape=(cells, packed, cells, shape(2, 64, 16,...]
    unnamed x26 -> x20, local copies, waits for them, and re-layouts: 10.4 us -> 8.56 us
    reshape x2 -> x0, local copies, waits for them, and re-layouts: 1.52 us -> none  [the longest x1 0.84 us: on_device(): jnp.pad(out_weight.reshape(256, HEADS, 64), ((0, 0), (0, 0), (64, 0)))]
where the time goes in v2:
time: 104 us
  Pallas kernels  94.7 us (91%)
  local copies, waits for them, and re-layouts  8.56 us (8%)
    pallas_call x1, Pallas kernels, on_device(): pl.pallas_call(kernel, out_shape=(cells, packed, cells, shape(2, 64, 16,...  93.1 us
    unnamed x20, local copies, waits for them, and re-layouts  8.56 us

profile of v2, /device:TPU:1, one launch (start us, length us, event | category | flops | bytes accessed | tf_op | source)
XLA Modules:
  0.0 104.0 jit_solution(4132990976231984965)
XLA Ops:
  0.6 0.0 copy-start.9
  0.7 0.6 copy-done.9
  1.3 0.0 copy-start
  1.3 1.0 copy-done
  2.3 0.0 copy-start.1
  2.3 1.0 copy-done.1
  3.3 0.0 copy-start.2
  3.3 0.9 copy-done.2
  4.2 0.0 copy-start.3
  4.2 0.9 copy-done.3
  5.2 0.0 copy-start.4
  5.2 0.9 copy-done.4
  6.1 0.0 copy-start.5
  6.1 0.9 copy-done.5
  7.0 0.0 copy-start.6
  7.0 0.8 copy-done.6
  7.8 0.0 copy-start.7
  7.8 0.7 copy-done.7
  8.5 0.0 copy-start.8
  8.5 0.7 copy-done.8
  9.2 93.1 %unet_step.1 = (bf16[8,128,128]{2,1,0:T(8,128)(2,1)S(1)}, f32[8,32,256]{2,1,0:T(8,128)S(1)}, bf16[8,128,128]{2,1,0:T(8,128)(2,1)S(1)}, bf16[2,64,16,128]{3,2,1,0:T(8,128)(2,1)S(1)}, bf16[96,16,128]{2,1,0:T(8,128)(2,1)S(1)}) custom-call(s32[8]{0:T(128)S(1)} %copy-done.9, bf16[8,32,256]{2,1,0:T(8,128)(2,1)S(1)} %bitcast.24, bf16[8,128,128]{2,1,0:T(8,128)(2,1)S(1)} %bitcast.22, ...), custom_call_target="tpu_custom_call" | custom-call | tf_op jit(solution)/shard_map/unet_step/pallas_call | solution.py:633
  102.3 1.6 %unpack.1 = (bf16[8,128,128]{2,1,0:T(8,128)(2,1)}, f32[8,32,256]{2,1,0:T(8,128)}, bf16[8,128,128]{2,1,0:T(8,128)(2,1)}, f32[768,256]{1,0:T(8,128)}, f32[256,256]...) custom-call(bf16[8,128,128]{2,1,0:T(8,128)(2,1)S(1)} %get-tuple-element.23.d, ...), custom_call_target="tpu_custom_call" | custom-call | tf_op jit(solution)/shard_map/unpack/pallas_call | solution.py:657
Async XLA Ops:
  0.6 0.7 copy-start.9
  1.3 1.0 copy-start
  2.3 1.0 copy-start.1
  3.3 0.9 copy-start.2
  4.2 0.9 copy-start.3
  5.2 0.9 copy-start.4
  6.1 0.9 copy-start.5
  7.0 0.8 copy-start.6
  7.8 0.7 copy-start.7
  8.5 0.7 copy-start.8

commit v3 on v2

--- a/solution.py
+++ b/solution.py
@@ -16,6 +16,7 @@
 CHUNK = 1024
 TAPS = [(-1, -1), (-1, 0), (-1, 1), (0, -1), (0, 0), (0, 1), (1, -1), (1, 0), (1, 1)]
 VMEM = pl.BlockSpec(memory_space=pltpu.VMEM)
+ANY = pl.BlockSpec(memory_space=pltpu.HBM)
 
 
 def nn(a, b):
@@ -55,9 +56,10 @@
 
 
 def kernel(
+    noise_hbm, x_hbm, skip_hbm, cot_hbm, wqkv_hbm, wout_hbm, wup_hbm, wconv_hbm, fscale_hbm, fshift_hbm,
+    dec_ref, gb_ref, gskip_ref, eag, lag,
     noise, x_ref, skip_ref, cot_ref, wqkv, wout, wup, wconv, fscale, fshift,
-    dec_ref, gb_ref, gskip_ref, eag, lag,
-    woutn, wq, wkv, kv_send, q_send, kv_in, q_fold, q_in, v1, xall, s_ref, p_ref, invl_ref, o_buf, o_send, o_fold,
+    woutn, wq, wkv, kv_send, q_send, kv_in, q_fold, q_in, v1, xall, s_ref, top_ref, p_ref, invl_ref, o_buf, o_send, o_fold,
     ocell, gx, hx, gt, gedge, hedge, ghalo, hhalo, pre_ref, act_ref, dh_ref, dy_ref, du_ref,
     do_send, do_fold, ext_ref, qt_ref, dot_ref, dkvt, dq_acc, dq_send, dq_fold, dq_in, pair_send, pair_in, dkv_send,
     dkv_in, gacc, gkv, eg, epin, ehs, ersin, lg, lrs, sems,
@@ -68,10 +70,25 @@
     pair = lax.div(r, 2)
     kslot = pair * COLS + c
     head, quarter = lax.div(r, 4), lax.rem(r, 4)
-    qslot = quarter * COLS + c
-    own = head == quarter
+    zhi, group = lax.rem(pair, 2), lax.div(pair, 4)
+    qslot = lax.rem(pair, 4) * COLS + c
+    own = zhi == group
     spot = c * HEADS + head
-    cols = [lax.rem(c + j, COLS) for j in range(COLS)]
+    sign = 1 - 2 * par
+    cols = [lax.rem(c + COLS + sign * j, COLS) for j in range(COLS)]
+
+    def pair_at(i):
+        return lax.rem(pair + 8 + sign * i, 8)
+
+    loads = [
+        pltpu.make_async_copy(src, dst, sems.at[104 + i])
+        for i, (src, dst) in enumerate((
+            (x_hbm, x_ref), (wqkv_hbm, wqkv), (cot_hbm, cot_ref), (skip_hbm, skip_ref), (wout_hbm, wout),
+            (wup_hbm, wup), (wconv_hbm, wconv), (fscale_hbm, fscale), (fshift_hbm, fshift), (noise_hbm, noise),
+        ))
+    ]
+    for load in loads:
+        load.start()
 
     barrier = pltpu.get_barrier_semaphore()
 
@@ -91,7 +108,7 @@
     def to_attention(src, dst, send, recv):
         def row(i):
             h = lax.rem(head + i, HEADS)
-            dr = HEADS * h + head
+            dr = HEADS * h + 2 * group + par
             send_or_keep((i == 0) & own, src.at[c * HEADS + h], dst.at[qslot], send, recv, dr, c)
             for j in range(1, COLS):
                 remote(src.at[cols[j] * HEADS + h], dst.at[qslot], send, recv, dr, cols[j]).start()
@@ -99,7 +116,7 @@
         loop(0, HEADS, row)
 
     def to_cells(src, dst, send, recv, row):
-        dr = 4 * quarter + row
+        dr = 2 * (4 * zhi + row) + par
         send_or_keep(dr == r, src.at[row * COLS + c], dst.at[spot], send, recv, dr, c)
         for j in range(1, COLS):
             remote(src.at[row * COLS + cols[j]], dst.at[spot], send, recv, dr, cols[j]).start()
@@ -115,20 +132,21 @@
 
     def to_parity(lo, hi, source, target, send, recv, first=0, last=COLS):
         def row(i):
-            at = lax.rem(pair + i, 8)
+            at = pair_at(i)
             dr = 2 * at + par
+            got = recv(i) if callable(recv) else recv
             for j in range(first, last):
                 src = source(at, cols[j])
                 if j == 0:
-                    send_or_keep(i == 0, src, target, send, recv, dr, c)
+                    send_or_keep(i == 0, src, target, send, got, dr, c)
                 else:
-                    remote(src, target, send, recv, dr, cols[j]).start()
+                    remote(src, target, send, got, dr, cols[j]).start()
 
         loop(lo, hi, row)
 
     def halo_start(ext, edge, halo, base):
         up, down = lax.rem(r + ROWS - 1, ROWS), lax.rem(r + 1, ROWS)
-        left, right = cols[COLS - 1], cols[1]
+        left, right = lax.rem(c + COLS - 1, COLS), lax.rem(c + 1, COLS)
         copies = [
             remote(ext.at[:, 1, pl.ds(1, 2)], ext.at[:, 3, pl.ds(1, 2)], sems.at[base], sems.at[base + 1], up, c),
             remote(ext.at[:, 2, pl.ds(1, 2)], ext.at[:, 0, pl.ds(1, 2)], sems.at[base + 2], sems.at[base + 3], down, c),
@@ -198,7 +216,7 @@
         for j in range(1, COLS):
             remote(mine, mine, esem[4], esem[5], r, cols[j]).start()
         def row(i):
-            dr = 2 * lax.rem(pair + i, 8) + par
+            dr = 2 * pair_at(i) + par
             for j in range(COLS):
                 remote(mine, mine, esem[4], esem[5], dr, cols[j]).start()
 
@@ -241,6 +259,8 @@
 
         loop(0, 4, some)
 
+    loads[0].wait()
+    loads[1].wait()
     zero64 = jnp.zeros((64, 256), BF)
     for h in range(HEADS):
         wq[128 * h : 128 * h + 64] = (wqkv[64 * h : 64 * h + 64].astype(F32) * 0.125).astype(BF)
@@ -272,12 +292,16 @@
             gedge[1, a, pl.ds(s, 1), :] = g[64 * a + 63 : 64 * a + 64]
 
     pl.semaphore_wait(barrier, ROWS * COLS - 1)
+    to_attention(q_send, q_fold, sems.at[2], sems.at[3])
     to_parity(
-        0, 8, lambda at, dc: kv_send.at[dc * HEADS + lax.div(at, 2)], kv_in.at[par, kslot], sems.at[0], sems.at[1]
+        0, 8, lambda at, dc: kv_send.at[dc * HEADS + lax.div(at, 2)], kv_in.at[par, kslot], sems.at[0],
+        lambda i: sems.at[80 + i],
     )
-    to_attention(q_send, q_fold, sems.at[2], sems.at[3])
+    loads[2].wait()
     loop(0, 8, take_cot)
     cot_copies = halo_start(gx, gedge, ghalo, 16)
+    for load in loads[3:]:
+        load.wait()
 
     def take_skip(s):
         pre_ref[s] = nn(split, skip_ref[s])
@@ -287,7 +311,6 @@
         block = wout[:, 128 * g : 128 * (g + 1)].astype(F32)
         woutn[:, 256 * g : 256 * g + 128] = jnp.where(low_lane, 0.0, half_turn(block)).astype(BF)
         woutn[:, 256 * g + 128 : 256 * g + 256] = jnp.where(low_lane, 0.0, block).astype(BF)
-    halo_finish(gx, ghalo, cot_copies)
 
     def back_conv(half):
         total = jnp.zeros((512, 128), F32)
@@ -296,49 +319,53 @@
             total = total + nn(window, wconv[t])
         dh_ref[pl.ds(4 * half, 4)] = total.reshape(4, 128, 128)
 
-    loop(0, 2, back_conv)
-
-    drain(kv_in.at[par], sems.at[1])
-    mate_kv = remote(kv_in.at[par], kv_in.at[par], sems.at[4], sems.at[5], mate, c)
-    mate_kv.start()
     drain(q_fold, sems.at[3])
     unfold(q_fold, q_in, False, True)
+    top_ref[...] = jnp.full((1024, 128), -jnp.inf, F32)
+
+    def score(half, at):
+        part = kv_in[half, pl.ds(COLS * at, COLS)].reshape(256, 128)
+        place = pl.multiple_of(half * 2048 + at * 256, 256)
+        v1[pl.ds(place, 256), :] = jnp.where(low_lane, jnp.ones_like(part), part)
+        for b in range(4):
+            rows = slice(BLOCK * b, BLOCK * (b + 1))
+            s = nt(q_in[8 * b : 8 * b + 8].reshape(BLOCK, 128), part)
+            s_ref[rows, pl.ds(place, 256)] = s
+            top_ref[rows, :] = jnp.maximum(top_ref[rows, :], jnp.maximum(s[:, 0:128], s[:, 128:256]))
+
+    def mate_group(i):
+        at = kv_in.at[par, pl.ds(COLS * lax.rem(pair + 8 - sign * i, 8), COLS)]
+        return remote(at, at, sems.at[88 + i], sems.at[96 + i], mate, c)
+
+    def take_group(i):
+        at = lax.rem(pair + 8 - sign * i, 8)
+        drain(kv_in.at[par, pl.ds(COLS * at, COLS)], sems.at[80 + i])
+        mate_group(i).start()
+        score(par, at)
+
+    def take_mate(i):
+        mate_group(i).wait()
+        score(1 - par, pair_at(i))
+
+    take_group(0)
+
+    def both(i):
+        take_group(i)
+        take_mate(i - 1)
+
+    loop(1, 8, both)
+    to_parity(0, 8, lambda at, dc: x_ref.at[dc], xall.at[kslot], sems.at[60], sems.at[61], 0, 4)
+    take_mate(7)
     for _ in range(3):
         drain(kv_send.at[pl.ds(0, 21)], sems.at[0])
     drain32(q_send, sems.at[2])
 
-    def ones_values(half):
-        def some(i):
-            part = kv_in[half, pl.ds(i * 16, 16)].reshape(512, 128)
-            lane = lax.broadcasted_iota(jnp.int32, (512, 128), 1)
-            at = pl.multiple_of(half * 2048 + i * 512, 512)
-            v1[pl.ds(at, 512), :] = jnp.where(lane < 64, jnp.ones_like(part), part)
-
-        loop(0, 4, some)
-
-    ones_values(par)
-    mate_kv.wait()
-    ones_values(1 - par)
-    to_parity(0, 8, lambda at, dc: x_ref.at[dc], xall.at[par, kslot], sems.at[60], sems.at[61], 0, 4)
-
-    def keys(j):
-        n = CHUNK // 32
-        return kv_in[j * n // 64, (j * n) % 64 : (j * n) % 64 + n].reshape(CHUNK, 128)
-
     def forward(b):
-        q = q_in[pl.ds(8 * b, 8)].reshape(BLOCK, 128)
-        top = None
+        rows = pl.ds(pl.multiple_of(b * BLOCK, BLOCK), BLOCK)
+        m = jnp.max(top_ref[rows, :], axis=1, keepdims=True)
+        acc = jnp.zeros((BLOCK, 128), F32)
         for j in range(4096 // CHUNK):
-            s = nt(q, keys(j))
-            s_ref[:, CHUNK * j : CHUNK * (j + 1)] = s
-            for g in range(CHUNK // 128):
-                part = s[:, 128 * g : 128 * (g + 1)]
-                top = part if top is None else jnp.maximum(top, part)
-        m = jnp.max(top, axis=1, keepdims=True)
-        acc = jnp.zeros((BLOCK, 128), F32)
-        rows = pl.ds(pl.multiple_of(b * BLOCK, BLOCK), BLOCK)
-        for j in range(4096 // CHUNK):
-            p = jnp.exp(s_ref[:, CHUNK * j : CHUNK * (j + 1)] - m).astype(BF)
+            p = jnp.exp(s_ref[rows, CHUNK * j : CHUNK * (j + 1)] - m).astype(BF)
             p_ref[rows, CHUNK * j : CHUNK * (j + 1)] = p
             acc = acc + nn(p, v1[CHUNK * j : CHUNK * (j + 1), :])
         inv = 1.0 / jnp.where(low_lane, 1.0, half_turn(acc))
@@ -349,7 +376,8 @@
         to_cells(o_send, o_fold, sems.at[6], sems.at[7], b)
 
     loop(0, 1024 // BLOCK, forward)
-    to_parity(0, 8, lambda at, dc: x_ref.at[dc], xall.at[par, kslot], sems.at[60], sems.at[61], 4, 8)
+    halo_finish(gx, ghalo, cot_copies)
+    loop(0, 2, back_conv)
 
     levels = fscale.shape[0]
     level = lax.broadcasted_iota(jnp.int32, (levels, 128), 0)
@@ -362,7 +390,7 @@
     drain32(o_send, sems.at[6])
     unfold(o_fold, ocell, True, False)
     oc = ocell[...].reshape(8, HEADS, 32, 128)
-    branch = xt.astype(F32)
+    branch = x_ref[...].reshape(256, 256).astype(F32)
     for h in range(HEADS):
         branch = branch + nt(oc[:, h].reshape(256, 128), woutn[:, 128 * h : 128 * (h + 1)])
     y = branch.astype(BF)
@@ -402,6 +430,7 @@
         for s in range(8):
             do_send[s * HEADS + h] = do[s]
     to_attention(do_send, do_fold, sems.at[8], sems.at[9])
+    to_parity(0, 8, lambda at, dc: x_ref.at[dc], xall.at[kslot], sems.at[60], sems.at[61], 4, 8)
 
     early_put(120, scale_sum)
     early_put(122, shift_sum)
@@ -440,11 +469,6 @@
         eg[1, k - 64] = jnp.zeros((16, 128), BF)
     early_halves().start()
 
-    drain(xall.at[par], sems.at[61])
-    mate_x = remote(xall.at[par], xall.at[par], sems.at[62], sems.at[63], mate, c)
-    mate_x.start()
-    drain(xall.at[par, pl.ds(0, 63)], sems.at[60])
-
     drain(do_fold, sems.at[9])
     drain32(do_send, sems.at[8])
     unfold(do_fold, ocell, True, True)
@@ -468,7 +492,6 @@
     loop(0, 4, prepare)
     gkv[...] = jnp.zeros((256, 256), F32)
     early_scatter()
-    mate_x.wait()
 
     def backward(half, j):
         at = pl.multiple_of(half * 2048 + j * CHUNK, CHUNK)
@@ -481,27 +504,25 @@
             dq_acc[rows, :] += nn(ds, kc)
             part = nn(qt_ref[b], ds) + nn(dot_ref[b], p)
             dkvt[...] = part if b == 0 else dkvt[...] + part
-        xc = xall[half, pl.ds(32 * j, 32)].reshape(CHUNK, 256)
-        gkv[0:128] += nn(dkvt[...].astype(BF), xc)
-        return dkvt[...].T.reshape(32, 32, 128)
 
     def pair_copy(j):
-        at = pl.ds(32 * j, 32)
-        return remote(pair_send.at[at], pair_in.at[at], sems.at[10 + j], sems.at[12 + j], mate, c)
+        return remote(pair_send.at[j], pair_in.at[j], sems.at[10 + j], sems.at[12 + j], mate, c)
 
     def mate_chunk(j):
-        pair_send[pl.ds(32 * j, 32)] = backward(1 - par, j).astype(BF)
+        backward(1 - par, j)
+        pair_send[j] = dkvt[...].astype(BF)
         pair_copy(j).start()
 
     loop(0, 2, mate_chunk)
     early_gather()
-    zhi = lax.rem(pair, 2)
+    drain(xall, sems.at[61])
+    drain(xall.at[pl.ds(0, 63)], sems.at[60])
 
     def own_chunk(j):
-        part = backward(par, j)
+        backward(par, j)
         pair_copy(j).wait()
-        at = pl.ds(32 * j, 32)
-        dkv_send[at] = (part + pair_in[at].astype(F32)).astype(BF)
+        total = dkvt[...] + pair_in[j].astype(F32)
+        dkv_send[pl.ds(32 * j, 32)] = total.T.astype(BF).reshape(32, 32, 128)
         target = dkv_in.at[zhi, spot]
 
         def row(i):
@@ -512,6 +533,7 @@
                 remote(dkv_send.at[rp * COLS + cols[k]], target, sems.at[14], sems.at[15], dr, cols[k]).start()
 
         loop(0, 4, row)
+        gkv[0:128] += nn(total.astype(BF), xall[pl.ds(32 * j, 32)].reshape(CHUNK, 256))
 
     loop(0, 2, own_chunk)
 
@@ -520,7 +542,7 @@
         dq = dq_acc[rows, :]
         dq_send[pl.ds(8 * b, 8)] = fold_low(dq).astype(BF)
         to_cells(dq_send, dq_fold, sems.at[56], sems.at[57], b)
-        xq = xall[lax.rem(b, 2), pl.ds(COLS * (2 * quarter + lax.div(b, 2)), COLS)].reshape(BLOCK, 256)
+        xq = xall[pl.ds(COLS * (4 * zhi + b), COLS)].reshape(BLOCK, 256)
         gkv[128:256] += nn(dq.T.astype(BF), xq)
 
     loop(0, 4, give_dq)
@@ -531,11 +553,13 @@
             piece = (gkv[lo : lo + 64, lanes] * factor).astype(BF)
             lg[12 * g + 4 * part : 12 * g + 4 * part + 4] = piece.reshape(4, 16, 128)
 
+    member = quarter * COLS + c
+
     def send_lg(i):
         dr = HEADS * head + i
-        send_or_keep(quarter == i, lg.at[i * COLS + c], lrs.at[qslot], sems.at[58], sems.at[59], dr, c)
+        send_or_keep(quarter == i, lg.at[i * COLS + c], lrs.at[member], sems.at[58], sems.at[59], dr, c)
         for j in range(1, COLS):
-            remote(lg.at[i * COLS + cols[j]], lrs.at[qslot], sems.at[58], sems.at[59], dr, cols[j]).start()
+            remote(lg.at[i * COLS + cols[j]], lrs.at[member], sems.at[58], sems.at[59], dr, cols[j]).start()
 
     loop(0, 3, send_lg)
     early_drain()
@@ -545,8 +569,8 @@
     @pl.when(quarter < 3)
     def _():
         drain(lrs, sems.at[59])
-        mine = lag.at[head * 24 + qslot]
-        lag[head * 24 + qslot] = jnp.sum(lrs[...].astype(F32), axis=0).astype(BF)
+        mine = lag.at[head * 24 + member]
+        lag[head * 24 + member] = jnp.sum(lrs[...].astype(F32), axis=0).astype(BF)
         for j in range(1, COLS):
             remote(mine, mine, sems.at[64], sems.at[65], r, cols[j]).start()
 
@@ -586,28 +610,54 @@
         drain(lg, sems.at[58])
 
 
-def unpack(dec, gb, gskip, eag, lag, dec_ref, gb_ref, gskip_ref, gqkv_ref, gout_ref, gup_ref, gconv_ref, gscale_ref, gshift_ref):
-    dec_ref[...] = dec[...]
-    gb_ref[...] = gb[...]
-    gskip_ref[...] = gskip[...]
+def unpack(
+    dec, gb, gskip, eag, lag, dec_ref, gb_ref, gskip_ref, gqkv_ref, gout_ref, gup_ref, gconv_ref, gscale_ref, gshift_ref,
+    dec_v, gb_v, gskip_v, eag_v, lag_v, gqkv_v, gout_v, gup_v, gconv_v, gscale_v, gshift_v, sems,
+):
+    held = (dec_v, gb_v, gskip_v, eag_v, lag_v)
+    loads = [
+        pltpu.make_async_copy(src, dst, sems.at[i]) for i, (src, dst) in enumerate(zip((dec, gb, gskip, eag, lag), held))
+    ]
+    for load in loads:
+        load.start()
+    stores = [
+        pltpu.make_async_copy(src, dst, sems.at[5 + i])
+        for i, (src, dst) in enumerate((
+            (dec_v, dec_ref), (gb_v, gb_ref), (gskip_v, gskip_ref), (gconv_v, gconv_ref), (gscale_v, gscale_ref),
+            (gshift_v, gshift_ref), (gup_v, gup_ref), (gout_v, gout_ref), (gqkv_v, gqkv_ref),
+        ))
+    ]
+    loads[3].wait()
 
     def early(at, n):
-        return eag[at // 64, at % 64 : at % 64 + n].reshape(n * 16, 128).astype(F32)
+        return eag_v[at // 64, at % 64 : at % 64 + n].reshape(n * 16, 128).astype(F32)
 
     for t in range(9):
-        gconv_ref[t] = early(8 * t, 8)
-    levels = gscale_ref.shape[0]
-    gscale_ref[...] = early(120, 2)[0:levels]
-    gshift_ref[...] = early(122, 2)[0:levels]
+        gconv_v[t] = early(8 * t, 8)
+    stores[3].start()
+    levels = gscale_v.shape[0]
+    gscale_v[...] = early(120, 2)[0:levels]
+    gshift_v[...] = early(122, 2)[0:levels]
     for g in range(2):
         lanes = slice(128 * g, 128 * (g + 1))
-        gup_ref[:, lanes] = early(72 + 8 * g, 8)
-        gout_ref[:, lanes] = early(88 + 16 * g, 16)
+        gup_v[:, lanes] = early(72 + 8 * g, 8)
+        gout_v[:, lanes] = early(88 + 16 * g, 16)
+    for i in range(4, 8):
+        stores[i].start()
+    loads[4].wait()
+    for g in range(2):
+        lanes = slice(128 * g, 128 * (g + 1))
         for part in range(3):
             for h in range(HEADS):
                 at = 24 * h + 12 * g + 4 * part
                 rows = slice(256 * part + 64 * h, 256 * part + 64 * h + 64)
-                gqkv_ref[rows, lanes] = lag[at : at + 4].reshape(64, 128).astype(F32)
+                gqkv_v[rows, lanes] = lag_v[at : at + 4].reshape(64, 128).astype(F32)
+    stores[8].start()
+    for i in range(3):
+        loads[i].wait()
+        stores[i].start()
+    for store in stores:
+        store.wait()
 
 
 def on_device(
@@ -633,24 +683,26 @@
     parts = pl.pallas_call(
         kernel,
         out_shape=(cells, packed, cells, shape(2, 64, 16, 128, kind=BF), shape(96, 16, 128, kind=BF)),
-        in_specs=[pl.BlockSpec(memory_space=pltpu.SMEM)] + [VMEM] * 9,
+        in_specs=[ANY] * 10,
         out_specs=(VMEM,) * 5,
         scratch_shapes=[
+            pltpu.SMEM((8,), jnp.int32), bf(8, 32, 256), bf(8, 128, 128), bf(8, 128, 128), bf(768, 256), bf(256, 256),
+            bf(128, 256), bf(9, 128, 128), f32(levels, 128), f32(levels, 128),
             bf(256, 512), bf(512, 256), bf(512, 256), bf(*packet), bf(*folded), bf(2, 64, 32, 128), bf(*folded),
-            bf(*packet), bf(4096, 128), bf(2, 64, 32, 256), f32(BLOCK, 4096), bf(1024, 4096), f32(1024, 128),
+            bf(*packet), bf(4096, 128), bf(64, 32, 256), f32(1024, 4096), f32(1024, 128), bf(1024, 4096), f32(1024, 128),
             bf(1024, 128), bf(*folded), bf(*folded),
             bf(*packet), bf(8, 4, 4, 32, 128), bf(8, 4, 4, 32, 128), bf(8, 128, 128),
             f32(2, 2, 8, 128), f32(2, 2, 8, 128), f32(2, 3, 2, 8, 128), f32(2, 3, 2, 8, 128),
             f32(8, 128, 128), f32(8, 128, 128), f32(8, 128, 128), f32(256, 256), f32(256, 128),
             bf(*folded), bf(*folded), bf(1024, 128), bf(4, 128, 256), bf(4, 128, 256), f32(128, CHUNK),
             f32(1024, 128), bf(*folded), bf(*folded), bf(*packet),
-            bf(64, 32, 128), bf(64, 32, 128), bf(64, 32, 128), bf(2, 32, 32, 128), f32(9, 128, 128), f32(256, 256),
+            bf(2, 128, CHUNK), bf(2, 128, CHUNK), bf(64, 32, 128), bf(2, 32, 32, 128), f32(9, 128, 128), f32(256, 256),
             bf(2, 64, 16, 128), bf(64, 16, 128), bf(64, 16, 128), bf(64, 16, 128),
             bf(24, 16, 128), bf(32, 16, 128),
-            pltpu.SemaphoreType.DMA((72,)),
+            pltpu.SemaphoreType.DMA((120,)),
         ],
         compiler_params=pltpu.CompilerParams(
-            collective_id=0, has_side_effects=True, vmem_limit_bytes=44 * 1024 * 1024
+            collective_id=0, has_side_effects=True, vmem_limit_bytes=54 * 1024 * 1024
         ),
         name="unet_step",
     )(noise_level, x, skip, cot, qkv_weight, out_weight, up_weight, conv_weight, film_scale, film_shift)
@@ -660,9 +712,14 @@
             cells, packed, cells, shape(768, 256), shape(256, 256), shape(128, 256), shape(9, 128, 128),
             shape(levels, 128), shape(levels, 128),
         ),
-        in_specs=[VMEM] * 5,
-        out_specs=(VMEM,) * 9,
-        compiler_params=pltpu.CompilerParams(vmem_limit_bytes=16 * 1024 * 1024),
+        in_specs=[ANY] * 5,
+        out_specs=(ANY,) * 9,
+        scratch_shapes=[
+            bf(8, 128, 128), f32(8, 32, 256), bf(8, 128, 128), bf(2, 64, 16, 128), bf(96, 16, 128), f32(768, 256),
+            f32(256, 256), f32(128, 256), f32(9, 128, 128), f32(levels, 128), f32(levels, 128),
+            pltpu.SemaphoreType.DMA((14,)),
+        ],
+        compiler_params=pltpu.CompilerParams(vmem_limit_bytes=62 * 1024 * 1024),
         name="unpack",
     )(*parts)
     decoded, grad_x, grad_skip = outs[:3]

time: 104 us -> 94.5 us (0.909)
  local copies, waits for them, and re-layouts: 8.56 us -> 0 us
    unnamed x20 -> x0, local copies, waits for them, and re-layouts: 8.56 us -> none
    pallas_call x1, Pallas kernels: 93.1 us -> 90.8 us  [on_device(): pl.pallas_call(kernel, out_shape=(cells, packed, cells, shape(2, 64, 16,...]
    pallas_call x1, Pallas kernels: 1.62 us -> 2.92 us  [on_device(): pl.pallas_call(unpack, out_shape=(cells, packed, cells, shape(768, 256),...]
where the time goes in v3:
time: 94.5 us; the launch traced here: 94.4 us
  Pallas kernels  93.7 us (99%)
    pallas_call x1, Pallas kernels, on_device(): pl.pallas_call(kernel, out_shape=(cells, packed, cells, shape(2, 64, 16,...  90.8 us
    pallas_call x1, Pallas kernels, on_device(): pl.pallas_call(unpack, out_shape=(cells, packed, cells, shape(768, 256),...  2.92 us

profile of v3, /device:TPU:1, one launch (start us, length us, event | category | flops | bytes accessed | tf_op | source)
XLA Modules:
  0.0 94.4 jit_solution(16381031030365536715)
XLA Ops:
  0.6 90.8 %unet_step.1 = (bf16[8,128,128]{2,1,0:T(8,128)(2,1)}, f32[8,32,256]{2,1,0:T(8,128)}, bf16[8,128,128]{2,1,0:T(8,128)(2,1)}, bf16[2,64,16,128]{3,2,1,0:T(8,128)(2,1)}, bf16[96,16,128]{2,1,0:T(8,128)(2,1)}) custom-call(s32[8]{0:T(128)} %noise_hbm.1, bf16[8,32,256]{2,1,0:T(8,128)(2,1)} %bitcast.24, bf16[8,128,128]{2,1,0:T(8,128)(2,1)} %bitcast.22, ...), custom_call_target="tpu_custom_call" | custom-call | tf_op jit(solution)/shard_map/unet_step/pallas_call | solution.py:683
  91.4 2.9 %unpack.1 = (bf16[8,128,128]{2,1,0:T(8,128)(2,1)}, f32[8,32,256]{2,1,0:T(8,128)}, bf16[8,128,128]{2,1,0:T(8,128)(2,1)}, f32[768,256]{1,0:T(8,128)}, f32[256,256]...) custom-call(bf16[8,128,128]{2,1,0:T(8,128)(2,1)} %get-tuple-element.23.dec, ...), custom_call_target="tpu_custom_call" | custom-call | tf_op jit(solution)/shard_map/unpack/pallas_call | solution.py:709

commit v4 on v3

--- a/solution.py
+++ b/solution.py
@@ -57,8 +57,8 @@
 
 def kernel(
     noise_hbm, x_hbm, skip_hbm, cot_hbm, wqkv_hbm, wout_hbm, wup_hbm, wconv_hbm, fscale_hbm, fshift_hbm,
-    dec_ref, gb_ref, gskip_ref, eag, lag,
-    noise, x_ref, skip_ref, cot_ref, wqkv, wout, wup, wconv, fscale, fshift,
+    dec_hbm, gb_hbm, gskip_hbm, eag_hbm, lag_hbm,
+    dec_ref, gb_ref, gskip_ref, eag, lag, noise, x_ref, skip_ref, cot_ref, wqkv, wout, wup, wconv, fscale, fshift,
     woutn, wq, wkv, kv_send, q_send, kv_in, q_fold, q_in, v1, xall, s_ref, top_ref, p_ref, invl_ref, o_buf, o_send, o_fold,
     ocell, gx, hx, gt, gedge, hedge, ghalo, hhalo, pre_ref, act_ref, dh_ref, dy_ref, du_ref,
     do_send, do_fold, ext_ref, qt_ref, dot_ref, dkvt, dq_acc, dq_send, dq_fold, dq_in, pair_send, pair_in, dkv_send,
@@ -445,24 +445,34 @@
 
     halo_finish(hx, hhalo, hid_copies)
 
-    def conv(half):
-        total = jnp.zeros((512, 128), F32)
+    def weight_grad(half):
         grads = [gt[4 * half + i] for i in range(4)]
         for t, (dr, dc) in enumerate(TAPS):
             window = hx[pl.ds(4 * half, 4), 1 + dr : 3 + dr, 1 + dc : 3 + dc]
-            total = total + nt(window.reshape(512, 128), wconv[t])
             term = None
             for i in range(4):
                 one = nn(grads[i], window[i].reshape(128, 128))
                 term = one if term is None else term + one
             gacc[t] = gacc[t] + term
+
+    def conv(half):
+        total = jnp.zeros((512, 128), F32)
+        for t, (dr, dc) in enumerate(TAPS):
+            window = hx[pl.ds(4 * half, 4), 1 + dr : 3 + dr, 1 + dc : 3 + dc]
+            total = total + nt(window.reshape(512, 128), wconv[t])
         low = total.astype(BF)
         for i in range(4):
             dec_ref[4 * half + i] = nn(merge, low[128 * i : 128 * (i + 1)]).astype(BF)
             gskip_ref[4 * half + i] = nn(merge, dh_ref[4 * half + i].astype(BF)).astype(BF)
 
     gacc[...] = jnp.zeros((9, 128, 128), F32)
-    loop(0, 2, conv)
+    loop(0, 2, weight_grad)
+
+    def turn_queries(b):
+        q = q_in[pl.ds(8 * b, 8)].reshape(BLOCK, 128)
+        qt_ref[b] = q.astype(F32).T[0:64].astype(BF)
+
+    loop(0, 4, turn_queries)
     for t in range(9):
         early_put(8 * t, gacc[t])
     for k in range(124, 128):
@@ -476,7 +486,6 @@
 
     def prepare(b):
         rows = pl.ds(pl.multiple_of(b * BLOCK, BLOCK), BLOCK)
-        q = q_in[pl.ds(8 * b, 8)].reshape(BLOCK, 128)
         do = (ocell[pl.ds(8 * b, 8)].reshape(BLOCK, 128).astype(F32) * invl_ref[rows, :]).astype(BF)
         dof = do.astype(F32)
         delta = -jnp.sum(dof * o_buf[rows, :].astype(F32), axis=1, keepdims=True)
@@ -485,8 +494,7 @@
         rest = delta - high - mid
         ext = jnp.where(lane == 0, high, jnp.where(lane == 1, mid, jnp.where(lane == 2, rest, dof)))
         ext_ref[rows, :] = ext.astype(BF)
-        qt_ref[b] = q.astype(F32).T.astype(BF)
-        dot_ref[b] = dof.T.astype(BF)
+        dot_ref[b] = dof.T[64:128].astype(BF)
         dq_acc[rows, :] = jnp.zeros((BLOCK, 128), F32)
 
     loop(0, 4, prepare)
@@ -502,8 +510,9 @@
             p = p_ref[rows, pl.ds(at, CHUNK)]
             ds = (p.astype(F32) * nt(ext_ref[rows, :], vc)).astype(BF)
             dq_acc[rows, :] += nn(ds, kc)
-            part = nn(qt_ref[b], ds) + nn(dot_ref[b], p)
-            dkvt[...] = part if b == 0 else dkvt[...] + part
+            for lo, lhs, rhs in ((0, qt_ref, ds), (64, dot_ref, p)):
+                part = nn(lhs[b], rhs)
+                dkvt[lo : lo + 64] = part if b == 0 else dkvt[lo : lo + 64] + part
 
     def pair_copy(j):
         return remote(pair_send.at[j], pair_in.at[j], sems.at[10 + j], sems.at[12 + j], mate, c)
@@ -514,9 +523,6 @@
         pair_copy(j).start()
 
     loop(0, 2, mate_chunk)
-    early_gather()
-    drain(xall, sems.at[61])
-    drain(xall.at[pl.ds(0, 63)], sems.at[60])
 
     def own_chunk(j):
         backward(par, j)
@@ -533,19 +539,16 @@
                 remote(dkv_send.at[rp * COLS + cols[k]], target, sems.at[14], sems.at[15], dr, cols[k]).start()
 
         loop(0, 4, row)
-        gkv[0:128] += nn(total.astype(BF), xall[pl.ds(32 * j, 32)].reshape(CHUNK, 256))
+        pair_send[j] = total.astype(BF)
 
     loop(0, 2, own_chunk)
 
-    def give_dq(b):
-        rows = pl.ds(pl.multiple_of(b * BLOCK, BLOCK), BLOCK)
-        dq = dq_acc[rows, :]
-        dq_send[pl.ds(8 * b, 8)] = fold_low(dq).astype(BF)
-        to_cells(dq_send, dq_fold, sems.at[56], sems.at[57], b)
+    drain(xall, sems.at[61])
+    drain(xall.at[pl.ds(0, 63)], sems.at[60])
+    gkv[0:128] = nn(pair_send[0], xall[0:32].reshape(CHUNK, 256)) + nn(pair_send[1], xall[32:64].reshape(CHUNK, 256))
+    for b in range(4):
         xq = xall[pl.ds(COLS * (4 * zhi + b), COLS)].reshape(BLOCK, 256)
-        gkv[128:256] += nn(dq.T.astype(BF), xq)
-
-    loop(0, 4, give_dq)
+        gkv[128:256] += nn(dq_acc[BLOCK * b : BLOCK * (b + 1), :].T.astype(BF), xq)
 
     for g in range(2):
         lanes = slice(128 * g, 128 * (g + 1))
@@ -554,6 +557,7 @@
             lg[12 * g + 4 * part : 12 * g + 4 * part + 4] = piece.reshape(4, 16, 128)
 
     member = quarter * COLS + c
+    kind = head * COLS + c
 
     def send_lg(i):
         dr = HEADS * head + i
@@ -562,25 +566,42 @@
             remote(lg.at[i * COLS + cols[j]], lrs.at[member], sems.at[58], sems.at[59], dr, cols[j]).start()
 
     loop(0, 3, send_lg)
+
+    def give_dq(b):
+        rows = pl.ds(pl.multiple_of(b * BLOCK, BLOCK), BLOCK)
+        dq_send[pl.ds(8 * b, 8)] = fold_low(dq_acc[rows, :]).astype(BF)
+        to_cells(dq_send, dq_fold, sems.at[56], sems.at[57], b)
+
+    loop(0, 4, give_dq)
+    early_gather()
+    loop(0, 2, conv)
+    stores = [
+        pltpu.make_async_copy(src, dst, sems.at[68 + i])
+        for i, (src, dst) in enumerate((
+            (dec_ref, dec_hbm), (gskip_ref, gskip_hbm), (gb_ref, gb_hbm), (eag, eag_hbm), (lag, lag_hbm),
+        ))
+    ]
+    stores[0].start()
+    stores[1].start()
+
+    @pl.when(quarter < 3)
+    def _():
+        drain(lrs, sems.at[59])
+        mine = lag.at[quarter * 32 + kind]
+        lag[quarter * 32 + kind] = jnp.sum(lrs[...].astype(F32), axis=0).astype(BF)
+        for j in range(1, COLS):
+            remote(mine, mine, sems.at[64], sems.at[65], r, cols[j]).start()
+
+        def row(i):
+            dr = 2 * pair_at(i) + par
+            for j in range(COLS):
+                remote(mine, mine, sems.at[64], sems.at[65], dr, cols[j]).start()
+
+        loop(1, 8, row)
+
     early_drain()
     last_swap = early_swap()
     last_swap.start()
-
-    @pl.when(quarter < 3)
-    def _():
-        drain(lrs, sems.at[59])
-        mine = lag.at[head * 24 + member]
-        lag[head * 24 + member] = jnp.sum(lrs[...].astype(F32), axis=0).astype(BF)
-        for j in range(1, COLS):
-            remote(mine, mine, sems.at[64], sems.at[65], r, cols[j]).start()
-
-        def row(i):
-            dr = lax.rem(r + i, ROWS)
-            for j in range(COLS):
-                remote(mine, mine, sems.at[64], sems.at[65], dr, cols[j]).start()
-
-        loop(1, ROWS, row)
-
     drain(dq_fold, sems.at[57])
     drain32(dq_send, sems.at[56])
     unfold(dq_fold, dq_in, False, False)
@@ -594,20 +615,46 @@
         grad = grad + nn(dq_all[:, h].reshape(256, 128), wq[rows, :])
         grad = grad + nn(dkv_all[:, h].reshape(256, 128), wkv[rows, :])
     gb_ref[...] = grad.reshape(8, 32, 256)
+    stores[2].start()
     last_swap.wait()
+    stores[3].start()
 
     @pl.when(quarter < 3)
     def _():
-        drain(lag.at[pl.ds(0, 95)], sems.at[65])
         drain(lg.at[pl.ds(0, 23)], sems.at[58])
-        for _ in range(3):
-            drain(lrs, sems.at[64])
+        drain(lrs, sems.at[64])
         drain(lrs.at[pl.ds(0, 31)], sems.at[64])
 
     @pl.when(quarter == 3)
     def _():
-        drain(lag, sems.at[65])
         drain(lg, sems.at[58])
+        drain(lag.at[pl.ds(0, 32)], sems.at[65])
+
+    @pl.when(quarter == 1)
+    def _():
+        drain(lag.at[pl.ds(0, 31)], sems.at[65])
+
+    def forward_sums(at):
+        part = lag.at[pl.ds(at, 32)]
+        remote(part, part, sems.at[66], sems.at[67], mate, c).start()
+
+    @pl.when(par == 0)
+    def _():
+        drain(lag.at[pl.ds(0, 63)], sems.at[65])
+        forward_sums(0)
+        forward_sums(64)
+        drain(lag.at[pl.ds(0, 64)], sems.at[66])
+        drain(lag.at[pl.ds(0, 32)], sems.at[67])
+
+    @pl.when(par == 1)
+    def _():
+        forward_sums(32)
+        drain(lag.at[pl.ds(0, 32)], sems.at[66])
+        drain(lag.at[pl.ds(0, 64)], sems.at[67])
+
+    stores[4].start()
+    for store in stores:
+        store.wait()
 
 
 def unpack(
@@ -649,7 +696,8 @@
         lanes = slice(128 * g, 128 * (g + 1))
         for part in range(3):
             for h in range(HEADS):
-                at = 24 * h + 12 * g + 4 * part
+                piece = 12 * g + 4 * part
+                at = 32 * (piece // 8) + 8 * h + piece % 8
                 rows = slice(256 * part + 64 * h, 256 * part + 64 * h + 64)
                 gqkv_v[rows, lanes] = lag_v[at : at + 4].reshape(64, 128).astype(F32)
     stores[8].start()
@@ -684,8 +732,9 @@
         kernel,
         out_shape=(cells, packed, cells, shape(2, 64, 16, 128, kind=BF), shape(96, 16, 128, kind=BF)),
         in_specs=[ANY] * 10,
-        out_specs=(VMEM,) * 5,
+        out_specs=(ANY,) * 5,
         scratch_shapes=[
+            bf(8, 128, 128), f32(8, 32, 256), bf(8, 128, 128), bf(2, 64, 16, 128), bf(96, 16, 128),
             pltpu.SMEM((8,), jnp.int32), bf(8, 32, 256), bf(8, 128, 128), bf(8, 128, 128), bf(768, 256), bf(256, 256),
             bf(128, 256), bf(9, 128, 128), f32(levels, 128), f32(levels, 128),
             bf(256, 512), bf(512, 256), bf(512, 256), bf(*packet), bf(*folded), bf(2, 64, 32, 128), bf(*folded),
@@ -694,7 +743,7 @@
             bf(*packet), bf(8, 4, 4, 32, 128), bf(8, 4, 4, 32, 128), bf(8, 128, 128),
             f32(2, 2, 8, 128), f32(2, 2, 8, 128), f32(2, 3, 2, 8, 128), f32(2, 3, 2, 8, 128),
             f32(8, 128, 128), f32(8, 128, 128), f32(8, 128, 128), f32(256, 256), f32(256, 128),
-            bf(*folded), bf(*folded), bf(1024, 128), bf(4, 128, 256), bf(4, 128, 256), f32(128, CHUNK),
+            bf(*folded), bf(*folded), bf(1024, 128), bf(4, 64, 256), bf(4, 64, 256), f32(128, CHUNK),
             f32(1024, 128), bf(*folded), bf(*folded), bf(*packet),
             bf(2, 128, CHUNK), bf(2, 128, CHUNK), bf(64, 32, 128), bf(2, 32, 32, 128), f32(9, 128, 128), f32(256, 256),
             bf(2, 64, 16, 128), bf(64, 16, 128), bf(64, 16, 128), bf(64, 16, 128),

time: 94.5 us -> 92.8 us (0.982)
  Pallas kernels: 93.7 us -> 91.9 us
    pallas_call x1, Pallas kernels: 90.8 us -> 89 us  [on_device(): pl.pallas_call(kernel, out_shape=(cells, packed, cells, shape(2, 64, 16,...]
where the time goes in v4:
time: 92.8 us; the launch traced here: 92.6 us
  Pallas kernels  91.9 us (99%)
    pallas_call x1, Pallas kernels, on_device(): pl.pallas_call(kernel, out_shape=(cells, packed, cells, shape(2, 64, 16,...  89 us
    pallas_call x1, Pallas kernels, on_device(): pl.pallas_call(unpack, out_shape=(cells, packed, cells, shape(768, 256),...  2.92 us

profile of v4, /device:TPU:1, one launch (start us, length us, event | category | flops | bytes accessed | tf_op | source)
XLA Modules:
  0.0 92.6 jit_solution(5470837014963023983)
XLA Ops:
  0.6 89.0 %unet_step.1 = (bf16[8,128,128]{2,1,0:T(8,128)(2,1)}, f32[8,32,256]{2,1,0:T(8,128)}, bf16[8,128,128]{2,1,0:T(8,128)(2,1)}, bf16[2,64,16,128]{3,2,1,0:T(8,128)(2,1)}, bf16[96,16,128]{2,1,0:T(8,128)(2,1)}) custom-call(s32[8]{0:T(128)} %noise_hbm.1, bf16[8,32,256]{2,1,0:T(8,128)(2,1)} %bitcast.24, bf16[8,128,128]{2,1,0:T(8,128)(2,1)} %bitcast.22, ...), custom_call_target="tpu_custom_call" | custom-call | tf_op jit(solution)/shard_map/unet_step/pallas_call | solution.py:731
  89.7 2.9 %unpack.1 = (bf16[8,128,128]{2,1,0:T(8,128)(2,1)}, f32[8,32,256]{2,1,0:T(8,128)}, bf16[8,128,128]{2,1,0:T(8,128)(2,1)}, f32[768,256]{1,0:T(8,128)}, f32[256,256]...) custom-call(bf16[8,128,128]{2,1,0:T(8,128)(2,1)} %get-tuple-element.23.dec, ...), custom_call_target="tpu_custom_call" | custom-call | tf_op jit(solution)/shard_map/unpack/pallas_call | solution.py:758

commit v5 on v4

--- a/solution.py
+++ b/solution.py
@@ -323,39 +323,45 @@
     unfold(q_fold, q_in, False, True)
     top_ref[...] = jnp.full((1024, 128), -jnp.inf, F32)
 
-    def score(half, at):
-        part = kv_in[half, pl.ds(COLS * at, COLS)].reshape(256, 128)
-        place = pl.multiple_of(half * 2048 + at * 256, 256)
-        v1[pl.ds(place, 256), :] = jnp.where(low_lane, jnp.ones_like(part), part)
+    def score(groups):
+        parts = []
+        for half, at in groups:
+            part = kv_in[half, pl.ds(COLS * at, COLS)].reshape(256, 128)
+            place = pl.multiple_of(half * 2048 + at * 256, 256)
+            v1[pl.ds(place, 256), :] = jnp.where(low_lane, jnp.ones_like(part), part)
+            parts.append((part, place))
         for b in range(4):
             rows = slice(BLOCK * b, BLOCK * (b + 1))
-            s = nt(q_in[8 * b : 8 * b + 8].reshape(BLOCK, 128), part)
-            s_ref[rows, pl.ds(place, 256)] = s
-            top_ref[rows, :] = jnp.maximum(top_ref[rows, :], jnp.maximum(s[:, 0:128], s[:, 128:256]))
+            q = q_in[8 * b : 8 * b + 8].reshape(BLOCK, 128)
+            top = top_ref[rows, :]
+            for part, place in parts:
+                s = nt(q, part)
+                s_ref[rows, pl.ds(place, 256)] = s
+                top = jnp.maximum(top, jnp.maximum(s[:, 0:128], s[:, 128:256]))
+            top_ref[rows, :] = top
 
     def mate_group(i):
         at = kv_in.at[par, pl.ds(COLS * lax.rem(pair + 8 - sign * i, 8), COLS)]
         return remote(at, at, sems.at[88 + i], sems.at[96 + i], mate, c)
 
+    def own_at(i):
+        return lax.rem(pair + 8 - sign * i, 8)
+
     def take_group(i):
-        at = lax.rem(pair + 8 - sign * i, 8)
-        drain(kv_in.at[par, pl.ds(COLS * at, COLS)], sems.at[80 + i])
+        drain(kv_in.at[par, pl.ds(COLS * own_at(i), COLS)], sems.at[80 + i])
         mate_group(i).start()
-        score(par, at)
-
-    def take_mate(i):
-        mate_group(i).wait()
-        score(1 - par, pair_at(i))
 
     take_group(0)
+    score([(par, own_at(0))])
 
     def both(i):
         take_group(i)
-        take_mate(i - 1)
+        mate_group(i - 1).wait()
+        score([(par, own_at(i)), (1 - par, pair_at(i - 1))])
 
     loop(1, 8, both)
-    to_parity(0, 8, lambda at, dc: x_ref.at[dc], xall.at[kslot], sems.at[60], sems.at[61], 0, 4)
-    take_mate(7)
+    mate_group(7).wait()
+    score([(1 - par, pair_at(7))])
     for _ in range(3):
         drain(kv_send.at[pl.ds(0, 21)], sems.at[0])
     drain32(q_send, sems.at[2])
@@ -364,10 +370,10 @@
         rows = pl.ds(pl.multiple_of(b * BLOCK, BLOCK), BLOCK)
         m = jnp.max(top_ref[rows, :], axis=1, keepdims=True)
         acc = jnp.zeros((BLOCK, 128), F32)
-        for j in range(4096 // CHUNK):
-            p = jnp.exp(s_ref[rows, CHUNK * j : CHUNK * (j + 1)] - m).astype(BF)
-            p_ref[rows, CHUNK * j : CHUNK * (j + 1)] = p
-            acc = acc + nn(p, v1[CHUNK * j : CHUNK * (j + 1), :])
+        for j in range(4096 // 512):
+            p = jnp.exp(s_ref[rows, 512 * j : 512 * (j + 1)] - m).astype(BF)
+            p_ref[rows, 512 * j : 512 * (j + 1)] = p
+            acc = acc + nn(p, v1[512 * j : 512 * (j + 1), :])
         inv = 1.0 / jnp.where(low_lane, 1.0, half_turn(acc))
         invl_ref[rows, :] = inv
         o = jnp.where(low_lane, 0.0, acc * inv)
@@ -376,6 +382,7 @@
         to_cells(o_send, o_fold, sems.at[6], sems.at[7], b)
 
     loop(0, 1024 // BLOCK, forward)
+    to_parity(0, 8, lambda at, dc: x_ref.at[dc], xall.at[kslot], sems.at[60], sems.at[61], 0, 4)
     halo_finish(gx, ghalo, cot_copies)
     loop(0, 2, back_conv)
 
@@ -674,6 +681,9 @@
             (gshift_v, gshift_ref), (gup_v, gup_ref), (gout_v, gout_ref), (gqkv_v, gqkv_ref),
         ))
     ]
+    for i in range(3):
+        loads[i].wait()
+        stores[i].start()
     loads[3].wait()
 
     def early(at, n):
@@ -701,9 +711,6 @@
                 rows = slice(256 * part + 64 * h, 256 * part + 64 * h + 64)
                 gqkv_v[rows, lanes] = lag_v[at : at + 4].reshape(64, 128).astype(F32)
     stores[8].start()
-    for i in range(3):
-        loads[i].wait()
-        stores[i].start()
     for store in stores:
         store.wait()
 

time: 92.8 us -> 89.9 us (0.969)
  Pallas kernels: 91.9 us -> 89.1 us
    pallas_call x1, Pallas kernels: 89 us -> 86.4 us  [on_device(): pl.pallas_call(kernel, out_shape=(cells, packed, cells, shape(2, 64, 16,...]
where the time goes in v5:
time: 89.9 us; the launch traced here: 89.7 us
  Pallas kernels  89.1 us (99%)
    pallas_call x1, Pallas kernels, on_device(): pl.pallas_call(kernel, out_shape=(cells, packed, cells, shape(2, 64, 16,...  86.4 us
    pallas_call x1, Pallas kernels, on_device(): pl.pallas_call(unpack, out_shape=(cells, packed, cells, shape(768, 256),...  2.66 us

profile of v5, /device:TPU:1, one launch (start us, length us, event | category | flops | bytes accessed | tf_op | source)
XLA Modules:
  0.0 89.7 jit_solution(12874302922641623767)
XLA Ops:
  0.6 86.4 %unet_step.1 = (bf16[8,128,128]{2,1,0:T(8,128)(2,1)}, f32[8,32,256]{2,1,0:T(8,128)}, bf16[8,128,128]{2,1,0:T(8,128)(2,1)}, bf16[2,64,16,128]{3,2,1,0:T(8,128)(2,1)}, bf16[96,16,128]{2,1,0:T(8,128)(2,1)}) custom-call(s32[8]{0:T(128)} %noise_hbm.1, bf16[8,32,256]{2,1,0:T(8,128)(2,1)} %bitcast.24, bf16[8,128,128]{2,1,0:T(8,128)(2,1)} %bitcast.22, ...), custom_call_target="tpu_custom_call" | custom-call | tf_op jit(solution)/shard_map/unet_step/pallas_call | solution.py:738
  87.1 2.7 %unpack.1 = (bf16[8,128,128]{2,1,0:T(8,128)(2,1)}, f32[8,32,256]{2,1,0:T(8,128)}, bf16[8,128,128]{2,1,0:T(8,128)(2,1)}, f32[768,256]{1,0:T(8,128)}, f32[256,256]...) custom-call(bf16[8,128,128]{2,1,0:T(8,128)(2,1)} %get-tuple-element.23.dec, ...), custom_call_target="tpu_custom_call" | custom-call | tf_op jit(solution)/shard_map/unpack/pallas_call | solution.py:765
